TPU v7x, 1024 devices: a whole 4x8x16 slice. The times are simulated.
1024 devices in a mesh: ctx: 16 (over z), head: 64 (over x, y, core).
Axes of the slice: x: 4, y: 8, z: 16, core: 2. Of those that a mesh axis runs over, the one named last changes fastest.
Arguments:
- out_grad: bfloat16 [6144, 8192], P('ctx', 'head'), may hold values from -0.1796875 to 0.1796875
- conv_input: bfloat16 [6144, 8192], P('ctx', 'head'), may hold values from -0.119628906 to 0.119628906
- residues: float32 [16, 8192], P(None, 'head'), may hold values from -1.5 to 1.5
- decay_rate: float32 [16, 8192], P(None, 'head'), may hold values from 1e-05 to 0.033
- segments: int32 [6144], replicated, may hold values from 0 to 3, never falling along the last dimension, each value on 1 to 3072 neighbouring positions
- w_in: bfloat16 [8192, 8192], P('head'), may hold values from -0.0625 to 0.0625
Outputs:
- d_input: bfloat16 [6144, 8192], P('ctx', 'head')
- filter_grad: float32 [16, 8192], P(None, 'head')
Inputs may be any that keep to these rules, and one draw needn't show every extreme that they name: `segments`: document numbers never fall along the tokens; every document has 1 to 3072 tokens and one has exactly 3072.
All inputs are finite; a program needn't handle non-finite values.
Results may differ from a plain program's by a relative error of at most 0.0049.
Values may be sent and summed in bfloat16 or wider, within the bound.
No kernel may reach another device: no remote copies, remote signals or barrier semaphores. Data moves between devices by JAX's collectives and lax.ppermute only.
A program may use at most 32 MiB of HBM per device.

v0:
```python
import math

import jax
import jax.numpy as jnp
from jax import lax
from jax.sharding import PartitionSpec as P


def carried_in(part, axis, combine, identity):
    count = lax.axis_size(axis)
    place = lax.axis_index(axis)
    ahead = count - 1 - place
    gathered = jax.tree.map(lambda a: lax.all_gather(a, axis), part)
    state = jax.tree.map(lambda a, e: jnp.zeros_like(a) + jnp.asarray(e, a.dtype), part, identity)

    def one(hop, state):
        source = count - 1 - hop
        return combine(
            state, jax.tree.map(lambda a: lax.dynamic_index_in_dim(a, source, 0, False), gathered)
        )

    return lax.fori_loop(0, ahead, one, state)


def local(out_grad, conv_input, residues, decay_rate, segments, w_in):
    tok_rows = out_grad.shape[0]
    chan_width = out_grad.shape[1]
    mode_count = residues.shape[0]
    seq_total = segments.shape[0]
    ctx_index = lax.axis_index("ctx")
    row_start = ctx_index * tok_rows
    seg_own = lax.dynamic_slice_in_dim(segments, row_start, tok_rows)
    next_start = jnp.minimum(row_start + tok_rows, seq_total - 1)
    seg_next = lax.dynamic_slice_in_dim(segments, next_start, 1)[0]
    block_len = math.gcd(tok_rows, 32)
    block_count = tok_rows // block_len
    offsets = jnp.arange(block_len, dtype=jnp.float32)
    rising = jnp.exp(-offsets[:, None, None] * decay_rate[None])
    falling = jnp.exp(offsets[:, None, None] * decay_rate[None])
    grad_rows = out_grad.astype(jnp.float32).reshape(block_count, block_len, chan_width)
    weighted = (grad_rows[:, :, None, :] * rising[None]).reshape(
        block_count, block_len, mode_count * chan_width
    )
    seg_blocks = seg_own.reshape(block_count, block_len)
    ahead_mask = jnp.arange(block_len)[None, :] >= jnp.arange(block_len)[:, None]
    upper_mask = (ahead_mask[None] & (seg_blocks[:, :, None] == seg_blocks[:, None, :])).astype(
        jnp.float32
    )
    summed = jnp.einsum("bst,btk->bsk", upper_mask, weighted, precision=lax.Precision.HIGHEST)
    within = summed.reshape(block_count, block_len, mode_count, chan_width) * falling[None]
    next_first = jnp.concatenate([seg_blocks[1:, 0], seg_next[None]])
    linked = (seg_blocks == next_first[:, None]).astype(jnp.float32)
    tail_gain = jnp.exp(-(block_len - offsets)[:, None, None] * decay_rate[None])
    step_decay = jnp.exp(-block_len * decay_rate)

    def chain_step(state, scan_items):
        start_value, start_link = scan_items
        return (start_value + start_link * step_decay * state, state)

    zero_state = jnp.zeros((mode_count, chan_width), jnp.float32)
    head_value, following = lax.scan(
        chain_step, zero_state, (within[:, 0], linked[:, 0]), reverse=True
    )
    local_part = within + linked[:, :, None, None] * tail_gain[None] * following[:, None]
    local_part = local_part.reshape(tok_rows, mode_count, chan_width)
    position = jnp.arange(tok_rows, dtype=jnp.float32)
    reach_mask = (seg_own == seg_next).astype(jnp.float32)
    carry_gain = reach_mask[:, None, None] * jnp.exp(
        -(tok_rows - position)[:, None, None] * decay_rate[None]
    )
    through = jnp.exp(-tok_rows * decay_rate) * (seg_own[0] == seg_next).astype(jnp.float32)
    inputs = conv_input.astype(jnp.float32)
    base_filter = jnp.einsum("sc,smc->mc", inputs, local_part)
    carry_filter = jnp.einsum("sc,smc->mc", inputs, carry_gain)

    def compose(first_part, second_part):
        return (second_part[0] * first_part[0], second_part[1] + second_part[0] * first_part[1])

    unit_state = jnp.ones((mode_count, chan_width), jnp.float32)
    incoming = carried_in((through, head_value), "ctx", compose, (unit_state, zero_state))[1]
    filter_grad = lax.psum(base_filter + carry_filter * incoming, "ctx")
    adjoint = local_part + carry_gain * incoming[None]
    conv_grad = jnp.sum(residues[None] * adjoint, axis=1).astype(jnp.bfloat16)
    d_input = lax.dot_general(
        lax.all_gather(conv_grad, "head", axis=1, tiled=True),
        w_in,
        (((1,), (1,)), ((), ())),
        preferred_element_type=jnp.float32,
    )
    return (d_input.astype(jnp.bfloat16), filter_grad)


def solution(mesh):
    placed = (
        P("ctx", "head"),
        P("ctx", "head"),
        P(None, "head"),
        P(None, "head"),
        P(),
        P("head", None),
    )
    return jax.shard_map(
        local,
        mesh=mesh,
        in_specs=placed,
        out_specs=(P("ctx", "head"), P(None, "head")),
        check_vma=False,
    )
```

profile of v0, /device:TPU:1, one launch (start us, length us, event | category | flops | bytes accessed | tf_op | source)
XLA Modules:
  0.0 222.4 jit_solution(5676183581877505815)
XLA Ops:
  7.2 1.5 dynamic_slice.42
  8.7 1.5 compare_convert_fusion
  10.9 0.8 pad_add_fusion
  13.1 2.8 %mul.212 = f32[12,32,16,128]{3,2,1,0:T(8,128)} broadcast(bf16[12,32,128]{2,1,0:T(8,128)(2,1)} %bitcast.88), dimensions={0,1,3} | broadcast | bytes 3244032 | tf_op jit(solution)/shard_map/mul | solution.py:41
  15.9 4.6 %mul.213 = f32[12,32,2048]{2,1,0:T(8,128)} reshape(f32[12,32,16,128]{3,2,1,0:T(8,128)} %mul.212) | data formatting | bytes 6291456 | tf_op jit(solution)/shard_map/mul | solution.py:41
  20.7 3.8 %fusion.2 = f32[12,32,2048]{2,1,0:T(8,128)S(1)} fusion(f32[12,32,2048]{2,1,0:T(8,128)} %mul.213, f32[32,2048]{1,0:T(8,128)S(1)} %multiply_exponential_fusion.2, s32[12,32]{1,0:T(8,128)S(1)} %eq.40, pred[32,32]{1,0:T(8,128)(4,1)S(1)} %iota_compare_fusion), kind=kOutput, calls=%fused_computation.12 | convolution fusion | flops 302800896 | bytes 6556160 | tf_op jit(solution)/shard_map/bst,btk->bsk/dot_general | solution.py:49
  25.3 1.6 copy-done.1
  26.9 16.9 %while.32 = (s32[]{:T(128)}, f32[16,128]{1,0:T(8,128)S(1)}, f32[12,16,128]{2,1,0:T(8,128)S(1)}, f32[12,16,128]{2,1,0:T(8,128)S(1)}, f32[12]{0:T(128)S(1)}, /*ind...) while((s32[]{:T(128)}, f32[16,128]{1,0:T(8,128)S(1)}, f32[12,16,128]{2,1,0:T(8,128)S(1)}, ...), condition=%wide.region_1.2_spmd.clone, body=%wide.region_0.1_spmd.clone.sunk | while | flops 10244 | bytes 49292 | solution.py:61
  27.6 0.7 bitcast_add_fusion.2
  29.0 0.7 bitcast_add_fusion.2
  30.4 0.7 bitcast_add_fusion.2
  31.8 0.7 bitcast_add_fusion.2
  33.2 0.7 bitcast_add_fusion.2
  34.6 0.7 bitcast_add_fusion.2
  36.0 0.7 bitcast_add_fusion.2
  37.4 0.7 bitcast_add_fusion.2
  40.2 0.7 bitcast_add_fusion.2
  43.9 36.6 %all-gather = f32[256,128]{1,0:T(8,128)S(1)} all-gather(f32[16,128]{1,0:T(8,128)S(1)} %get-tuple-element.210), channel_id=2, replica_groups=mesh['ctx'=16,'head'=64] {'ctx'}, dimensions={0}, use_global_device_ids=true | all-gather | bytes 139264 | tf_op jit(solution)/shard_map/all_gather | solution.py:13
  80.5 19.6 %all-gather.1 = f32[256,128]{1,0:T(8,128)S(1)} all-gather(f32[16,128]{1,0:T(8,128)S(1)} %get-tuple-element.261), channel_id=3, replica_groups=mesh['ctx'=16,'head'=64] {'ctx'}, dimensions={0}, use_global_device_ids=true | all-gather | bytes 139264 | tf_op jit(solution)/shard_map/all_gather | solution.py:13
  100.8 4.8 %multiply_reduce_fusion.2 = bf16[384,128]{1,0:T(8,128)(2,1)} fusion(f32[16,128]{1,0:T(8,128)S(1)} %get-tuple-element.211, f32[16,128]{1,0:T(8,128)S(1)} %copy-done.2, f32[384]{0:T(512)S(1)} %subtract_negate_fusion, f32[384]{0:T(512)S(1)} %get-tuple-element.257, f32[12,16,128]{2,1,0:T(8,128)S(1)} %get-tuple-element.209, f32[48,8,16,128]{3,2,1,0:T(8,128)} %copy-done.1, ...), kind=kLoop, calls=%fused_computation.10 | loop fusion | flops 7815168 | bytes 3895808 | tf_op jit(solution)/shard_map/reduce_sum | solution.py:83
  105.6 3.7 %multiply_reduce_fusion.1 = (f32[128,16]{0,1:T(8,128)S(1)}, f32[128,16]{0,1:T(8,128)S(1)}) fusion(f32[128,384]{0,1:T(8,128)S(1)} %bitcast_convert_fusion, f32[12,16,128]{2,1,0:T(8,128)S(1)} %get-tuple-element.209, f32[48,8,16,128]{3,2,1,0:T(8,128)} %copy-done.1, f32[32,16,128]{2,1,0:T(8,128)S(1)} %get-tuple-element.259, f32[384]{0:T(512)S(1)} %compare_convert_fusion.1, ...), kind=kLoop, calls=%fused_computation.9 | loop fusion | flops 7860224 | bytes 3994112 | tf_op jit(solution)/shard_map/sc,smc->mc/dot_general | solution.py:73
  109.3 22.6 %psum.7 = f32[16,128]{1,0:T(8,128)} all-reduce(f32[16,128]{1,0:T(8,128)S(1)} %fusion.11), channel_id=1, replica_groups=mesh['ctx'=16,'head'=64] {'ctx'}, use_global_device_ids=true, to_apply=%region_5.6 | all-reduce | flops 2048 | bytes 16384 | tf_op jit(solution)/shard_map/psum | solution.py:81
  131.8 78.5 %all-gather.4.cloned.1.call-done = bf16[384,8192]{1,0:T(8,128)(2,1)} async-done(((bf16[384,128]{1,0:T(8,128)(2,1)}), bf16[384,8192]{1,0:T(8,128)(2,1)}) %all-gather.4.cloned.1.call-update) | async-done | bytes 6291472 | tf_op jit(solution)/shard_map/all_gather | solution.py:85
  210.3 5.2 %convolution_convert_fusion = bf16[384,128]{1,0:T(8,128)(2,1)} fusion(bf16[384,8192]{1,0:T(8,128)(2,1)} %all-gather.4.cloned.1.call-done, bf16[128,8192]{1,0:T(8,128)(2,1)S(1)} %copy-done), kind=kOutput, calls=%fused_computation.15 | convolution fusion | flops 805355520 | bytes 8486912 | tf_op jit(solution)/shard_map/dot_general | solution.py:84
  (76 shorter events, 13.0 us)
Async XLA Ops:
  7.2 203.2 %copy-start = (bf16[128,8192]{1,0:T(8,128)(2,1)S(1)}, bf16[128,8192]{1,0:T(8,128)(2,1)}, u32[]{:S(2)}) copy-start(bf16[128,8192]{1,0:T(8,128)(2,1)} %param.15) | copy-start | bytes 6291460
  7.2 203.1 %all-gather.4.cloned.1.call-start = ((), (), s32[]{:S(2)}) async-start(), calls=%async_computation | async-start | bytes 6389760 | tf_op jit(solution)/shard_map/all_gather | solution.py:85
  15.9 4.6 %copy-start.2 = (f32[16,128]{1,0:T(8,128)S(1)}, f32[16,128]{1,0:T(8,128)}, u32[]{:S(2)}) copy-start(f32[16,128]{1,0:T(8,128)} %param.13) | copy-start | bytes 24580
  24.5 76.3 %copy-start.4 = (f32[16,128]{1,0:T(8,128)S(1)}, f32[16,128]{1,0:T(8,128)}, u32[]{:S(2)}) copy-start(f32[16,128]{1,0:T(8,128)} %param.12) | copy-start | bytes 24580
  25.2 1.7 copy-start.1
  25.2 80.4 %copy-start.3 = (bf16[384,128]{1,0:T(8,128)(2,1)S(1)}, bf16[384,128]{1,0:T(8,128)(2,1)}, u32[]{:S(2)}) copy-start(bf16[384,128]{1,0:T(8,128)(2,1)} %param.11) | copy-start | bytes 294916
Sparse Core Ops, SparseCore 0:
  105.7 104.6 all-gather.3
where the time goes:
time: 223 us; the launch traced here: 222 us
  blocking collectives  78.8 us (35%)
  waiting for transfers between devices  78.5 us (35%)
  local copies, waits for them, and re-layouts  20 us (9%)
  other arithmetic  19.7 us (9%)
  between operations  15.5 us (7%)
  matrix products  9.01 us (4%)
    all_gather x1, waiting for transfers between devices, local(): lax.all_gather(conv_grad, 'head', axis=1, tiled=True)  78.5 us
    all_gather x2, blocking collectives, carried_in(): gathered = jax.tree.map(lambda a: lax.all_gather(a, axis), part)  56.3 us
    psum x1, blocking collectives, local(): filter_grad = lax.psum(base_filter + carry_filter * incoming, 'ctx')  22.6 us
    add x12, other arithmetic, chain_step(): return (start_value + start_link * step_decay * state, state)  8.34 us
    dynamic_slice x12, local copies, waits for them, and re-layouts, local(): lax.scan(chain_step, zero_state, (within[:, 0], linked[:, 0]), reverse=True)  8.03 us
    mul x2, local copies, waits for them, and re-layouts, local(): grad_rows[:, :, None, :] * rising[None]  7.39 us
    dot_general x1, matrix products, local(): lax.dot_general(lax.all_gather(conv_grad, 'head', axis=1, tiled=True), w_...  5.21 us
    reduce_sum x1, other arithmetic, local(): conv_grad = jnp.sum(residues[None] * adjoint, axis=1).astype(jnp.bfloat16)  4.76 us
  transfers between devices with their start and end apart: 1, of which 1 were waited for; matrix products, arithmetic and copies ran while one was open for 2% of the time, Pallas kernels for 0%

commit v1 on v0

v1 whole, which is shorter than its diff:
```python
import jax
import jax.numpy as jnp
from jax import lax
from jax.experimental import pallas as pl
from jax.experimental.pallas import tpu as pltpu
from jax.sharding import Mesh, PartitionSpec as P


LANES = 128
SUB = 8
F32 = jnp.float32
BF16 = jnp.bfloat16

VM = pl.BlockSpec(memory_space=pltpu.VMEM)
SM = pl.BlockSpec(memory_space=pltpu.SMEM)
HB = pl.BlockSpec(memory_space=pl.ANY)


def scan_kernel(
    shards, fan_x, fan_y,
    seg_ref, g_ref, x_ref, res_ref, rate_ref, w_ref,
    heads_ref, base_ref, parts_ref, keep_ref, give_ref, first_ref,
    gf, xf, prod, head_v, w_v, w_sem, ws_sem, head_sem,
):
    rows = g_ref.shape[0]
    base = lax.axis_index("z") * rows
    w_in = pltpu.make_async_copy(w_ref, w_v, w_sem)
    w_in.start()
    gf[...] = g_ref[...].astype(F32)
    xf[...] = x_ref[...].astype(F32)
    decay = jnp.exp(-rate_ref[...])
    d0, d1 = decay[:SUB], decay[SUB:]
    r0, r1 = res_ref[:SUB], res_ref[SUB:]
    zero = jnp.zeros((SUB, LANES), F32)
    one = jnp.ones((SUB, LANES), F32)

    def block(i, carry):
        a0, a1, f0, f1, g0, g1, c0, c1, nxt, run, first = carry
        top = rows - 16 * (i + 1)
        for k in range(15, -1, -1):
            t = top + k
            seg = seg_ref[base + t]
            same = seg == nxt
            nxt = seg
            run = jnp.logical_and(run, same)
            first = jnp.where(run, t, first)
            link = jnp.where(same, 1.0, 0.0).astype(F32)
            e0, e1 = d0 * link, d1 * link
            g = row(gf, t)
            x = row(xf, t)
            a0 = g + e0 * a0
            a1 = g + e1 * a1
            g0 = e0 * g0
            g1 = e1 * g1
            f0 = f0 + x * a0
            f1 = f1 + x * a1
            c0 = c0 + x * g0
            c1 = c1 + x * g1
            prod[pl.ds(pl.multiple_of(t * SUB, SUB), SUB), :] = r0 * a0 + r1 * a1
        return a0, a1, f0, f1, g0, g1, c0, c1, nxt, run, first

    last = seg_ref[base + rows - 1]
    init = (zero, zero, zero, zero, one, one, zero, zero, last, jnp.bool_(True), jnp.int32(rows - 1))
    a0, a1, f0, f1, _, _, c0, c1, _, _, first = lax.fori_loop(0, rows // 16, block, init)
    head_v[:SUB] = a0
    head_v[SUB:] = a1
    heads = [
        pltpu.make_async_copy(head_v, heads_ref.at[i], head_sem.at[i]) for i in range(shards)
    ]
    for c in heads:
        c.start()
    w_in.wait()
    width = w_v.shape[1] // (2 * fan_x * fan_y)
    mine = lax.axis_index("c")
    here = lax.axis_index("x")
    splits = []
    for k in range(fan_x):
        to = lax.rem(here + k, fan_x)
        for y in range(fan_y):
            for other, dst in ((0, keep_ref), (1, give_ref)):
                core = 1 - mine if other else mine
                at = pl.multiple_of(((to * fan_y + y) * 2 + core) * width, width)
                splits.append(
                    pltpu.make_async_copy(
                        w_v.at[:, pl.ds(at, width)],
                        dst.at[k, :, pl.ds(y * width, width)],
                        ws_sem.at[(k * fan_y + y) * 2 + other],
                    )
                )
    for c in splits:
        c.start()
    parts_ref[:SUB] = f0
    parts_ref[SUB : 2 * SUB] = f1
    parts_ref[2 * SUB : 3 * SUB] = c0
    parts_ref[3 * SUB :] = c1

    def fold(i, _):
        at = pl.multiple_of(i * 16, 16)
        total = prod[pl.ds(at * SUB, 16, stride=SUB), :]
        for k in range(1, SUB):
            total = total + prod[pl.ds(at * SUB + k, 16, stride=SUB), :]
        base_ref[pl.ds(at, 16), :] = total
        return 0

    lax.fori_loop(0, rows // 16, fold, 0)
    first_ref[...] = jnp.full((SUB, LANES), first, jnp.int32)
    for c in heads + splits:
        c.wait()


def marks_kernel(shards, rows, seg_ref, marks_ref):
    for i in range(shards):
        begin = seg_ref[i * rows]
        end = seg_ref[i * rows + rows - 1]
        whole = jnp.where(begin == end, 1.0, 0.0).astype(F32)
        marks_ref[pl.ds(i, 1), :] = jnp.full((1, LANES), whole, F32)
        if i + 1 < shards:
            on = jnp.where(end == seg_ref[(i + 1) * rows], 1.0, 0.0).astype(F32)
        else:
            on = jnp.float32(0.0)
        marks_ref[pl.ds(shards + i, 1), :] = jnp.full((1, LANES), on, F32)


def row(ref, at):
    return ref[pl.ds(at, SUB, stride=0), :]


def chain(heads_ref, marks_ref, rate, rows, visit):
    shards = heads_ref.shape[0]
    leap = jnp.exp(-float(rows) * rate)
    l0, l1 = leap[:SUB], leap[SUB:]
    in0 = in1 = jnp.zeros((SUB, LANES), F32)
    for i in range(shards - 1, -1, -1):
        visit(i, in0, in1)
        if i:
            whole = row(marks_ref, i)
            on = row(marks_ref, shards + i - 1)
            in0 = on * (heads_ref[i, :SUB] + whole * l0 * in0)
            in1 = on * (heads_ref[i, SUB:] + whole * l1 * in1)


def finish_kernel(
    heads_ref, marks_ref, res_ref, rate_ref, base_ref, parts_ref, first_ref,
    pay_ref, taps_ref, amp_v, pay_v, pay_sem,
):
    rows = base_ref.shape[0]
    modes = res_ref.shape[0]
    me = lax.axis_index("z")
    own = [jnp.zeros((SUB, LANES), F32)] * 2

    def visit(i, in0, in1):
        own[0] = jnp.where(me == i, in0, own[0])
        own[1] = jnp.where(me == i, in1, own[1])

    chain(heads_ref, marks_ref, rate_ref[...], rows, visit)
    taps_ref[:SUB] = parts_ref[:SUB] + parts_ref[2 * SUB : 3 * SUB] * own[0]
    taps_ref[SUB:] = parts_ref[SUB : 2 * SUB] + parts_ref[3 * SUB :] * own[1]
    amp_v[:SUB] = own[0] * res_ref[:SUB]
    amp_v[SUB:] = own[1] * res_ref[SUB:]
    first = first_ref[...]
    place = lax.broadcasted_iota(jnp.int32, (SUB, LANES), 0)
    back = (SUB - place).astype(F32)
    steps, terms = [], []
    for m in range(modes):
        rate = row(rate_ref, m)
        steps.append(jnp.exp(rate * -float(SUB)))
        terms.append(row(amp_v, m) * jnp.exp(rate * -back))

    def tokens(i, terms):
        terms = list(terms)
        at = pl.multiple_of(rows - 16 * (i + 1), 16)
        halves = []
        for h in (1, 0):
            tree = list(terms)
            while len(tree) > 1:
                tree = [tree[k] + tree[k + 1] for k in range(0, len(tree), 2)]
            halves.append(jnp.where(place + (at + SUB * h) >= first, tree[0], 0.0))
            terms = [a * b for a, b in zip(terms, steps)]
        carry = jnp.concatenate([halves[1], halves[0]], axis=0)
        pay_v[pl.ds(at, 16), :] = (base_ref[pl.ds(at, 16), :] + carry).astype(BF16)
        return tuple(terms)

    lax.fori_loop(0, rows // 16, tokens, tuple(terms))
    pays = [
        pltpu.make_async_copy(pay_v, pay_ref.at[i], pay_sem.at[i]) for i in range(pay_ref.shape[0])
    ]
    for c in pays:
        c.start()
    for c in pays:
        c.wait()


def product_kernel(pay_ref, *refs):
    w_refs, out_ref, conv = refs[:-2], refs[-2], refs[-1]
    fan_x = len(w_refs)
    mine = lax.axis_index("c")
    here = lax.axis_index("x")
    for y in range(pay_ref.shape[0]):
        conv[:, y * LANES : (y + 1) * LANES] = pay_ref[y]
    for k in range(fan_x):
        pair = lax.dot_general(
            conv[...], w_refs[k][...], (((1,), (1,)), ((), ())), preferred_element_type=F32
        )
        to = 2 * lax.rem(here + fan_x - k, fan_x)
        out_ref[to + mine] = pair[:, :LANES].astype(BF16)
        out_ref[to + 1 - mine] = pair[:, LANES:].astype(BF16)


def sum_kernel(parts_ref, out_ref):
    total = parts_ref[0].astype(F32)
    for i in range(1, parts_ref.shape[0]):
        total = total + parts_ref[i].astype(F32)
    out_ref[...] = total.astype(BF16)


def cost(flops, nbytes):
    return pl.CostEstimate(flops=flops, bytes_accessed=nbytes, transcendentals=0)


def device(out_grad, conv_input, residues, decay_rate, segments, w_in):
    shards, fan_x, fan_y = (lax.axis_size(n) for n in ("z", "x", "y"))
    rows, chans = out_grad.shape
    modes = residues.shape[0]
    feats, depth = w_in.shape[0], w_in.shape[1] // (2 * fan_x)
    sem = pltpu.SemaphoreType.DMA
    whole = pltpu.CompilerParams(vmem_limit_bytes=67_000_000)
    small = pltpu.CompilerParams(vmem_limit_bytes=16 * 2**20)
    heads, base, parts, keep, give, first = pl.pallas_call(
        lambda *refs: scan_kernel(shards, fan_x, fan_y, *refs),
        name="scan",
        out_shape=(
            jax.ShapeDtypeStruct((shards, modes, chans), F32),
            jax.ShapeDtypeStruct((rows, chans), F32),
            jax.ShapeDtypeStruct((2 * modes, chans), F32),
            jax.ShapeDtypeStruct((fan_x, feats, depth), BF16),
            jax.ShapeDtypeStruct((fan_x, feats, depth), BF16),
            jax.ShapeDtypeStruct((SUB, chans), jnp.int32),
        ),
        in_specs=[SM, VM, VM, VM, VM, HB],
        out_specs=(HB, VM, VM, HB, HB, VM),
        scratch_shapes=[
            pltpu.VMEM((rows, chans), F32), pltpu.VMEM((rows, chans), F32),
            pltpu.VMEM((rows * SUB, chans), F32), pltpu.VMEM((modes, chans), F32),
            pltpu.VMEM(w_in.shape, BF16),
            sem(()), sem((2 * fan_x * fan_y,)), sem((shards,)),
        ],
        compiler_params=whole,
        cost_estimate=cost(10_000_000, 8_000_000),
    )(segments, out_grad, conv_input, residues, decay_rate, w_in)

    heads_in = lax.all_to_all(heads, "z", 0, 0)
    got = lax.ppermute(give, "c", [(0, 1), (1, 0)])
    weights = []
    for k in range(fan_x):
        pair = jnp.concatenate([keep[k], got[k]], axis=0)
        if k:
            pair = lax.ppermute(pair, "x", [(i, (i + k) % fan_x) for i in range(fan_x)])
        weights.append(pair)
    marks = pl.pallas_call(
        lambda *refs: marks_kernel(shards, rows, *refs),
        name="marks",
        out_shape=jax.ShapeDtypeStruct((2 * shards, chans), F32),
        in_specs=[SM], out_specs=VM,
        compiler_params=small,
        cost_estimate=cost(100_000, 20_000),
    )(segments)
    pay, taps = pl.pallas_call(
        finish_kernel,
        name="finish",
        out_shape=(
            jax.ShapeDtypeStruct((fan_y, rows, chans), BF16),
            jax.ShapeDtypeStruct((modes, chans), F32),
        ),
        in_specs=[VM] * 7, out_specs=(HB, VM),
        scratch_shapes=[pltpu.VMEM((modes, chans), F32), pltpu.VMEM((rows, chans), BF16), sem((fan_y,))],
        compiler_params=small,
        cost_estimate=cost(10_000_000, 1_000_000),
    )(heads_in, marks, residues, decay_rate, base, parts, first)
    pay_in = lax.all_to_all(pay, "y", 0, 0)
    for n in range(4):
        taps = taps + lax.ppermute(taps, "z", [(i, i ^ (1 << n)) for i in range(shards)])
    split = pl.pallas_call(
        product_kernel,
        name="product",
        out_shape=jax.ShapeDtypeStruct((2 * fan_x, rows, feats), BF16),
        in_specs=[VM] * (1 + fan_x), out_specs=VM,
        scratch_shapes=[pltpu.VMEM((rows, depth), BF16)],
        compiler_params=small,
        cost_estimate=cost(4 * rows * depth * fan_x * feats, 4_000_000),
    )(pay_in, *weights)
    split_in = lax.all_to_all(split, ("x", "c"), 0, 0)
    d_input = pl.pallas_call(
        sum_kernel,
        name="total",
        out_shape=jax.ShapeDtypeStruct((rows, feats), BF16),
        in_specs=[VM], out_specs=VM,
        compiler_params=small,
        cost_estimate=cost(1_000_000, 900_000),
    )(split_in)
    return d_input, taps


def solution(mesh):
    grid = (16, 4, 8, 2)
    fine = Mesh(mesh.devices.reshape(grid), ("z", "x", "y", "c"))
    head = ("x", "y", "c")
    return jax.shard_map(
        device,
        mesh=fine,
        in_specs=(P("z", head), P("z", head), P(None, head), P(None, head), P(), P(head, None)),
        out_specs=(P("z", head), P(None, head)),
        check_vma=False,
    )
```

time: 223 us -> 127 us (0.57)
  the two profiles are of different devices: /device:TPU:1 before, /device:TPU:10 now
where the time goes in v1:
time: 127 us; the launch traced here: 126 us
  starting transfers between devices  61.8 us (49%)
  waiting for transfers between devices  49.5 us (39%)
  Pallas kernels  10.6 us (8%)
  local copies, waits for them, and re-layouts  2.49 us (2%)
    ppermute x4, starting transfers between devices, device(): lax.ppermute(taps, 'z', [(i, i ^ 1 << n) for i in range(shards)])  19 us
    ppermute x3, waiting for transfers between devices, device(): pair = lax.ppermute(pair, 'x', [(i, (i + k) % fan_x) for i in range(fan_x)])  19 us
    all_to_all x1, starting transfers between devices, device(): heads_in = lax.all_to_all(heads, 'z', 0, 0)  18.9 us
    ppermute x4, waiting for transfers between devices, device(): lax.ppermute(taps, 'z', [(i, i ^ 1 << n) for i in range(shards)])  17.5 us
    all_to_all x1, waiting for transfers between devices, device(): heads_in = lax.all_to_all(heads, 'z', 0, 0)  13.1 us
    ppermute x3, starting transfers between devices, device(): pair = lax.ppermute(pair, 'x', [(i, (i + k) % fan_x) for i in range(fan_x)])  10.5 us
    all_to_all x1, starting transfers between devices, device(): pay_in = lax.all_to_all(pay, 'y', 0, 0)  7.56 us
    pallas_call x1, Pallas kernels, device(): pl.pallas_call(lambda *refs: scan_kernel(shards, fan_x, fan_y, *refs), na...  5.54 us
  transfers between devices with their start and end apart: 11, of which 8 were waited for; matrix products, arithmetic and copies ran while one was open for 1% of the time, Pallas kernels for 2%

profile of v1, /device:TPU:10, one launch (start us, length us, event | category | flops | bytes accessed | tf_op | source)
XLA Modules:
  0.0 125.9 jit_solution(3935987802885096021)
XLA Ops:
  0.7 5.5 %scan.1 = (f32[16,16,128]{2,1,0:T(8,128)}, f32[384,128]{1,0:T(8,128)}, f32[32,128]{1,0:T(8,128)}, bf16[4,128,1024]{2,1,0:T(8,128)(2,1)}, bf16[4,128,1024]{2,1,0:T(8,128)(2,1)}, /*index=5*/s32[8,128]{1,0:T(8,128)}) custom-call(s32[6144]{0:T(1024)} %refs_0_.3, bf16[384,128]{1,0:T(8,128)(2,1)} %refs_1_.1, bf16[384,128]{1,0:T(8,128)(2,1)} %refs_2_.1, ...), custom_call_target="tpu_custom_call" | custom-call | flops 10000000 | bytes 8000000 | tf_op jit(solution)/shard_map/scan/pallas_call | solution.py:228
  6.2 1.9 %collective-permute-start = (bf16[4,128,1024]{2,1,0:T(8,128)(2,1)}, bf16[4,128,1024]{2,1,0:T(8,128)(2,1)S(1)}, u32[]{:S(2)}, u32[]{:S(2)}) collective-permute-start(bf16[4,128,1024]{2,1,0:T(8,128)(2,1)} %get-tuple-element.16), channel_id=1, source_target_pairs={{0,1},{1,0},{2,3},{3,2},{4,5},{5,4},{6,7},{7,6},{8,9},{9,8},{10,11... | collective-permute-start | bytes 3145736 | tf_op jit(solution)/shard_map/ppermute | solution.py:252
  8.1 18.9 %all-to-all-start = ((f32[16,16,128]{2,1,0:T(8,128)}), f32[16,16,128]{2,1,0:T(8,128)S(1)}, u32[]{:S(2)}, u32[]{:S(2)}) async-start(f32[16,16,128]{2,1,0:T(8,128)} %get-tuple-element.10), calls=%async_computation | async-start | bytes 262144 | tf_op jit(solution)/shard_map/all_to_all | solution.py:251
  27.0 1.0 marks.1.marks_ref
  28.0 13.1 %all-to-all-done.heads_ref = f32[16,16,128]{2,1,0:T(8,128)S(1)} async-done(((f32[16,16,128]{2,1,0:T(8,128)}), f32[16,16,128]{2,1,0:T(8,128)S(1)}, u32[]{:S(2)}, u32[]{:S(2)}) %all-to-all-start) | async-done | bytes 131104 | tf_op jit(solution)/shard_map/all_to_all | solution.py:251
  41.1 0.9 copy-done
  43.4 1.3 %finish.1 = (bf16[8,384,128]{2,1,0:T(8,128)(2,1)}, f32[16,128]{1,0:T(8,128)S(1)}) custom-call(f32[16,16,128]{2,1,0:T(8,128)S(1)} %all-to-all-done.heads_ref, f32[32,128]{1,0:T(8,128)S(1)} %marks.1.marks_ref, f32[16,128]{1,0:T(8,128)S(1)} %copy-done.2, f32[16,128]{1,0:T(8,128)S(1)} %copy-done.3, f32[384,128]{1,0:T(8,128)S(1)} %copy-done, ...), custom_call_target="tpu_custom_call" | custom-call | flops 10000000 | bytes 1000000 | tf_op jit(solution)/shard_map/finish/pallas_call | solution.py:267
  44.8 7.6 %all-to-all-start.1 = ((bf16[8,384,128]{2,1,0:T(8,128)(2,1)}), bf16[8,384,128]{2,1,0:T(8,128)(2,1)S(1)}, u32[]{:S(2)}, u32[]{:S(2)}) async-start(bf16[8,384,128]{2,1,0:T(8,128)(2,1)} %get-tuple-element.14), calls=%async_computation.1 | async-start | bytes 1572864 | tf_op jit(solution)/shard_map/all_to_all | solution.py:279
  52.5 3.4 %collective-permute-start.1 = (bf16[256,1024]{1,0:T(8,128)(2,1)S(1)}, bf16[256,1024]{1,0:T(8,128)(2,1)S(1)}, u32[]{:S(2)}, u32[]{:S(2)}) collective-permute-start(bf16[256,1024]{1,0:T(8,128)(2,1)S(1)} %pad_maximum_fusion.1), channel_id=1, source_target_pairs={{0,16},{16,32},{32,48},{48,0},{1,17},{17,33},{33,49},{49,1},{2,18}... | collective-permute-start | bytes 1572872 | tf_op jit(solution)/shard_map/ppermute | solution.py:257
  56.0 3.0 %collective-permute-start.2 = (bf16[256,1024]{1,0:T(8,128)(2,1)S(1)}, bf16[256,1024]{1,0:T(8,128)(2,1)S(1)}, u32[]{:S(2)}, u32[]{:S(2)}) collective-permute-start(bf16[256,1024]{1,0:T(8,128)(2,1)S(1)} %pad_maximum_fusion.2), channel_id=1, source_target_pairs={{0,32},{16,48},{32,0},{48,16},{1,33},{17,49},{33,1},{49,17},{2,34}... | collective-permute-start | bytes 1572872 | tf_op jit(solution)/shard_map/ppermute | solution.py:257
  59.1 4.1 %collective-permute-start.3 = (bf16[256,1024]{1,0:T(8,128)(2,1)S(1)}, bf16[256,1024]{1,0:T(8,128)(2,1)S(1)}, u32[]{:S(2)}, u32[]{:S(2)}) collective-permute-start(bf16[256,1024]{1,0:T(8,128)(2,1)S(1)} %pad_maximum_fusion.3), channel_id=1, source_target_pairs={{0,48},{16,0},{32,16},{48,32},{1,49},{17,1},{33,17},{49,33},{2,50}... | collective-permute-start | bytes 1572872 | tf_op jit(solution)/shard_map/ppermute | solution.py:257
  63.2 6.1 %collective-permute-done.1.refs_1_ = bf16[256,1024]{1,0:T(8,128)(2,1)S(1)} collective-permute-done((bf16[256,1024]{1,0:T(8,128)(2,1)S(1)}, bf16[256,1024]{1,0:T(8,128)(2,1)S(1)}, u32[]{:S(2)}, u32[]{:S(2)}) %collective-permute-start.1) | collective-permute-done | bytes 524320 | tf_op jit(solution)/shard_map/ppermute | solution.py:257
  69.2 5.0 %collective-permute-done.2.refs_2_ = bf16[256,1024]{1,0:T(8,128)(2,1)S(1)} collective-permute-done((bf16[256,1024]{1,0:T(8,128)(2,1)S(1)}, bf16[256,1024]{1,0:T(8,128)(2,1)S(1)}, u32[]{:S(2)}, u32[]{:S(2)}) %collective-permute-start.2) | collective-permute-done | bytes 524320 | tf_op jit(solution)/shard_map/ppermute | solution.py:257
  74.2 8.0 %collective-permute-done.3.refs_3_ = bf16[256,1024]{1,0:T(8,128)(2,1)S(1)} collective-permute-done((bf16[256,1024]{1,0:T(8,128)(2,1)S(1)}, bf16[256,1024]{1,0:T(8,128)(2,1)S(1)}, u32[]{:S(2)}, u32[]{:S(2)}) %collective-permute-start.3) | collective-permute-done | bytes 524320 | tf_op jit(solution)/shard_map/ppermute | solution.py:257
  82.2 2.0 %product.1 = bf16[8,384,128]{2,1,0:T(8,128)(2,1)} custom-call(bf16[8,384,128]{2,1,0:T(8,128)(2,1)S(1)} %all-to-all-done.1.pay_ref, bf16[256,1024]{1,0:T(8,128)(2,1)S(1)} %pad_maximum_fusion.refs_0_, bf16[256,1024]{1,0:T(8,128)(2,1)S(1)} %collective-permute-done.1.refs_1_, bf16[256,1024]{1,0:T(8,128)(2,1)S(1)} %collective-permute-done.2.refs_2_, ...), custom_call_target="tpu_custom_call" | custom-call | flops 805306368 | bytes 4000000 | tf_op jit(solution)/shard_map/product/pallas_call | solution.py:282
  84.1 3.9 %all-to-all-start.2 = ((bf16[8,384,128]{2,1,0:T(8,128)(2,1)}), bf16[8,384,128]{2,1,0:T(8,128)(2,1)S(1)}, u32[]{:S(2)}, u32[]{:S(2)}) async-start(bf16[8,384,128]{2,1,0:T(8,128)(2,1)} %product.1), calls=%async_computation.2 | async-start | bytes 1572864 | tf_op jit(solution)/shard_map/all_to_all | solution.py:291
  88.1 4.7 %collective-permute-start.4 = (f32[16,128]{1,0:T(8,128)S(1)}, f32[16,128]{1,0:T(8,128)S(1)}, u32[]{:S(2)}, u32[]{:S(2)}) collective-permute-start(f32[16,128]{1,0:T(8,128)S(1)} %get-tuple-element.17), channel_id=1, source_target_pairs={{0,64},{64,0},{128,192},{192,128},{256,320},{320,256},{384,448},{4... | collective-permute-start | bytes 24584 | tf_op jit(solution)/shard_map/ppermute | solution.py:281
  92.8 1.6 %collective-permute-done.4 = f32[16,128]{1,0:T(8,128)S(1)} collective-permute-done((f32[16,128]{1,0:T(8,128)S(1)}, f32[16,128]{1,0:T(8,128)S(1)}, u32[]{:S(2)}, u32[]{:S(2)}) %collective-permute-start.4) | collective-permute-done | bytes 8224 | tf_op jit(solution)/shard_map/ppermute | solution.py:281
  94.4 3.6 %collective-permute-start.5 = (f32[16,128]{1,0:T(8,128)S(1)}, f32[16,128]{1,0:T(8,128)S(1)}, u32[]{:S(2)}, u32[]{:S(2)}) collective-permute-start(f32[16,128]{1,0:T(8,128)S(1)} %add.12), channel_id=1, source_target_pairs={{0,128},{64,192},{128,0},{192,64},{256,384},{320,448},{384,256},{4... | collective-permute-start | bytes 24584 | tf_op jit(solution)/shard_map/ppermute | solution.py:281
  97.9 2.9 %collective-permute-done.5 = f32[16,128]{1,0:T(8,128)S(1)} collective-permute-done((f32[16,128]{1,0:T(8,128)S(1)}, f32[16,128]{1,0:T(8,128)S(1)}, u32[]{:S(2)}, u32[]{:S(2)}) %collective-permute-start.5) | collective-permute-done | bytes 8224 | tf_op jit(solution)/shard_map/ppermute | solution.py:281
  100.8 4.6 %collective-permute-start.6 = (f32[16,128]{1,0:T(8,128)S(1)}, f32[16,128]{1,0:T(8,128)S(1)}, u32[]{:S(2)}, u32[]{:S(2)}) collective-permute-start(f32[16,128]{1,0:T(8,128)S(1)} %add.13), channel_id=1, source_target_pairs={{0,256},{64,320},{128,384},{192,448},{256,0},{320,64},{384,128},{4... | collective-permute-start | bytes 24584 | tf_op jit(solution)/shard_map/ppermute | solution.py:281
  105.4 4.9 %collective-permute-done.6 = f32[16,128]{1,0:T(8,128)S(1)} collective-permute-done((f32[16,128]{1,0:T(8,128)S(1)}, f32[16,128]{1,0:T(8,128)S(1)}, u32[]{:S(2)}, u32[]{:S(2)}) %collective-permute-start.6) | collective-permute-done | bytes 8224 | tf_op jit(solution)/shard_map/ppermute | solution.py:281
  110.3 6.1 %collective-permute-start.7 = (f32[16,128]{1,0:T(8,128)S(1)}, f32[16,128]{1,0:T(8,128)S(1)}, u32[]{:S(2)}, u32[]{:S(2)}) collective-permute-start(f32[16,128]{1,0:T(8,128)S(1)} %add.14), channel_id=1, source_target_pairs={{0,512},{64,576},{128,640},{192,704},{256,768},{320,832},{384,896}... | collective-permute-start | bytes 24584 | tf_op jit(solution)/shard_map/ppermute | solution.py:281
  116.5 8.1 %collective-permute-done.7 = f32[16,128]{1,0:T(8,128)S(1)} collective-permute-done((f32[16,128]{1,0:T(8,128)S(1)}, f32[16,128]{1,0:T(8,128)S(1)}, u32[]{:S(2)}, u32[]{:S(2)}) %collective-permute-start.7) | collective-permute-done | bytes 8224 | tf_op jit(solution)/shard_map/ppermute | solution.py:281
  (27 shorter events, 3.1 us)
Async XLA Ops:
  0.6 26.4 %copy-start.1 = (s32[6144]{0:T(1024)S(1)}, s32[6144]{0:T(1024)}, u32[]{:S(2)}) copy-start(s32[6144]{0:T(1024)} %refs_0_.3) | copy-start | bytes 73732
  0.6 40.4 %copy-start.3 = (f32[16,128]{1,0:T(8,128)S(1)}, f32[16,128]{1,0:T(8,128)}, u32[]{:S(2)}) copy-start(f32[16,128]{1,0:T(8,128)} %rate_ref.1) | copy-start | bytes 24580
  0.7 40.4 %copy-start.2 = (f32[16,128]{1,0:T(8,128)S(1)}, f32[16,128]{1,0:T(8,128)}, u32[]{:S(2)}) copy-start(f32[16,128]{1,0:T(8,128)} %res_ref.1) | copy-start | bytes 24580
  6.2 46.2 %collective-permute-start = (bf16[4,128,1024]{2,1,0:T(8,128)(2,1)}, bf16[4,128,1024]{2,1,0:T(8,128)(2,1)S(1)}, u32[]{:S(2)}, u32[]{:S(2)}) collective-permute-start(bf16[4,128,1024]{2,1,0:T(8,128)(2,1)} %get-tuple-element.16), channel_id=1, source_target_pairs={{0,1},{1,0},{2,3},{3,2},{4,5},{5,4},{6,7},{7,6},{8,9},{9,8},{10,11... | collective-permute-start | bytes 3145736 | tf_op jit(solution)/shard_map/ppermute | solution.py:252
  8.1 33.0 %all-to-all-start = ((f32[16,16,128]{2,1,0:T(8,128)}), f32[16,16,128]{2,1,0:T(8,128)S(1)}, u32[]{:S(2)}, u32[]{:S(2)}) async-start(f32[16,16,128]{2,1,0:T(8,128)} %get-tuple-element.10), calls=%async_computation | async-start | bytes 262144 | tf_op jit(solution)/shard_map/all_to_all | solution.py:251
  41.1 0.9 copy-start
  42.0 0.7 copy-start.4
  42.7 0.7 copy-start.5
  43.4 8.9 %copy-start.6 = (bf16[4,128,1024]{2,1,0:T(8,128)(2,1)S(1)}, bf16[4,128,1024]{2,1,0:T(8,128)(2,1)}, u32[]{:S(2)}) copy-start(bf16[4,128,1024]{2,1,0:T(8,128)(2,1)} %get-tuple-element.15) | copy-start | bytes 3145732
  44.8 37.4 %all-to-all-start.1 = ((bf16[8,384,128]{2,1,0:T(8,128)(2,1)}), bf16[8,384,128]{2,1,0:T(8,128)(2,1)S(1)}, u32[]{:S(2)}, u32[]{:S(2)}) async-start(bf16[8,384,128]{2,1,0:T(8,128)(2,1)} %get-tuple-element.14), calls=%async_computation.1 | async-start | bytes 1572864 | tf_op jit(solution)/shard_map/all_to_all | solution.py:279
  52.5 16.7 %collective-permute-start.1 = (bf16[256,1024]{1,0:T(8,128)(2,1)S(1)}, bf16[256,1024]{1,0:T(8,128)(2,1)S(1)}, u32[]{:S(2)}, u32[]{:S(2)}) collective-permute-start(bf16[256,1024]{1,0:T(8,128)(2,1)S(1)} %pad_maximum_fusion.1), channel_id=1, source_target_pairs={{0,16},{16,32},{32,48},{48,0},{1,17},{17,33},{33,49},{49,1},{2,18}... | collective-permute-start | bytes 1572872 | tf_op jit(solution)/shard_map/ppermute | solution.py:257
  56.0 18.2 %collective-permute-start.2 = (bf16[256,1024]{1,0:T(8,128)(2,1)S(1)}, bf16[256,1024]{1,0:T(8,128)(2,1)S(1)}, u32[]{:S(2)}, u32[]{:S(2)}) collective-permute-start(bf16[256,1024]{1,0:T(8,128)(2,1)S(1)} %pad_maximum_fusion.2), channel_id=1, source_target_pairs={{0,32},{16,48},{32,0},{48,16},{1,33},{17,49},{33,1},{49,17},{2,34}... | collective-permute-start | bytes 1572872 | tf_op jit(solution)/shard_map/ppermute | solution.py:257
  59.1 23.1 %collective-permute-start.3 = (bf16[256,1024]{1,0:T(8,128)(2,1)S(1)}, bf16[256,1024]{1,0:T(8,128)(2,1)S(1)}, u32[]{:S(2)}, u32[]{:S(2)}) collective-permute-start(bf16[256,1024]{1,0:T(8,128)(2,1)S(1)} %pad_maximum_fusion.3), channel_id=1, source_target_pairs={{0,48},{16,0},{32,16},{48,32},{1,49},{17,1},{33,17},{49,33},{2,50}... | collective-permute-start | bytes 1572872 | tf_op jit(solution)/shard_map/ppermute | solution.py:257
  84.1 41.0 %all-to-all-start.2 = ((bf16[8,384,128]{2,1,0:T(8,128)(2,1)}), bf16[8,384,128]{2,1,0:T(8,128)(2,1)S(1)}, u32[]{:S(2)}, u32[]{:S(2)}) async-start(bf16[8,384,128]{2,1,0:T(8,128)(2,1)} %product.1), calls=%async_computation.2 | async-start | bytes 1572864 | tf_op jit(solution)/shard_map/all_to_all | solution.py:291
  88.1 6.3 %collective-permute-start.4 = (f32[16,128]{1,0:T(8,128)S(1)}, f32[16,128]{1,0:T(8,128)S(1)}, u32[]{:S(2)}, u32[]{:S(2)}) collective-permute-start(f32[16,128]{1,0:T(8,128)S(1)} %get-tuple-element.17), channel_id=1, source_target_pairs={{0,64},{64,0},{128,192},{192,128},{256,320},{320,256},{384,448},{4... | collective-permute-start | bytes 24584 | tf_op jit(solution)/shard_map/ppermute | solution.py:281
  94.4 6.4 %collective-permute-start.5 = (f32[16,128]{1,0:T(8,128)S(1)}, f32[16,128]{1,0:T(8,128)S(1)}, u32[]{:S(2)}, u32[]{:S(2)}) collective-permute-start(f32[16,128]{1,0:T(8,128)S(1)} %add.12), channel_id=1, source_target_pairs={{0,128},{64,192},{128,0},{192,64},{256,384},{320,448},{384,256},{4... | collective-permute-start | bytes 24584 | tf_op jit(solution)/shard_map/ppermute | solution.py:281
  100.8 9.5 %collective-permute-start.6 = (f32[16,128]{1,0:T(8,128)S(1)}, f32[16,128]{1,0:T(8,128)S(1)}, u32[]{:S(2)}, u32[]{:S(2)}) collective-permute-start(f32[16,128]{1,0:T(8,128)S(1)} %add.13), channel_id=1, source_target_pairs={{0,256},{64,320},{128,384},{192,448},{256,0},{320,64},{384,128},{4... | collective-permute-start | bytes 24584 | tf_op jit(solution)/shard_map/ppermute | solution.py:281
  110.3 14.2 %collective-permute-start.7 = (f32[16,128]{1,0:T(8,128)S(1)}, f32[16,128]{1,0:T(8,128)S(1)}, u32[]{:S(2)}, u32[]{:S(2)}) collective-permute-start(f32[16,128]{1,0:T(8,128)S(1)} %add.14), channel_id=1, source_target_pairs={{0,512},{64,576},{128,640},{192,704},{256,768},{320,832},{384,896}... | collective-permute-start | bytes 24584 | tf_op jit(solution)/shard_map/ppermute | solution.py:281

commit v2 on v1

v2 whole, which is shorter than its diff:
```python
import jax
import jax.numpy as jnp
from jax import lax
from jax.experimental import pallas as pl
from jax.experimental.pallas import tpu as pltpu
from jax.sharding import Mesh, PartitionSpec as P


LANES = 128
SUB = 8
F32 = jnp.float32
BF16 = jnp.bfloat16

VM = pl.BlockSpec(memory_space=pltpu.VMEM)
SM = pl.BlockSpec(memory_space=pltpu.SMEM)
HB = pl.BlockSpec(memory_space=pl.ANY)


def scan_kernel(
    shards, seg_ref, g_ref, x_ref, res_ref, rate_ref,
    ends_ref, base_ref, gf, xf, prod, end_v, end_sem,
):
    rows = g_ref.shape[0]
    base = lax.axis_index("z") * rows
    gf[...] = g_ref[...].astype(F32)
    xf[...] = x_ref[...].astype(F32)
    decay = jnp.exp(-rate_ref[...])
    d0, d1 = decay[:SUB], decay[SUB:]
    r0, r1 = res_ref[:SUB], res_ref[SUB:]
    zero = jnp.zeros((SUB, LANES), F32)
    one = jnp.ones((SUB, LANES), F32)

    def block(i, carry):
        a0, a1, f0, f1, g0, g1, c0, c1, nxt = carry
        top = rows - 16 * (i + 1)
        for k in range(15, -1, -1):
            t = top + k
            seg = seg_ref[base + t]
            link = jnp.where(seg == nxt, 1.0, 0.0).astype(F32)
            nxt = seg
            e0, e1 = d0 * link, d1 * link
            g = row(gf, t)
            x = row(xf, t)
            a0 = g + e0 * a0
            a1 = g + e1 * a1
            g0 = e0 * g0
            g1 = e1 * g1
            f0 = f0 + x * a0
            f1 = f1 + x * a1
            c0 = c0 + x * g0
            c1 = c1 + x * g1
            prod[pl.ds(pl.multiple_of(t * SUB, SUB), SUB), :] = r0 * a0 + r1 * a1
        return a0, a1, f0, f1, g0, g1, c0, c1, nxt

    init = (zero, zero, zero, zero, one, one, zero, zero, seg_ref[base + rows - 1])
    a0, a1, f0, f1, _, _, c0, c1, _ = lax.fori_loop(0, rows // 16, block, init)
    for n, pair in enumerate(((a0, a1), (f0, f1), (c0, c1))):
        end_v[16 * n : 16 * n + 16] = jnp.concatenate(pair, axis=0).astype(BF16)
    ends = [pltpu.make_async_copy(end_v, ends_ref.at[i], end_sem.at[i]) for i in range(shards)]
    for c in ends:
        c.start()

    def fold(i, _):
        at = pl.multiple_of(i * 16, 16)
        total = prod[pl.ds(at * SUB, 16, stride=SUB), :]
        for k in range(1, SUB):
            total = total + prod[pl.ds(at * SUB + k, 16, stride=SUB), :]
        base_ref[pl.ds(at, 16), :] = total
        return 0

    lax.fori_loop(0, rows // 16, fold, 0)
    for c in ends:
        c.wait()


def sort_kernel(shards, rows, fan_x, fan_y, seg_ref, w_ref, *refs):
    outs, (marks_ref, first_ref, out_sem) = refs[:fan_x], refs[fan_x:]
    feats = w_ref.shape[0]
    width = w_ref.shape[1] // (2 * fan_x * fan_y)
    mine = lax.axis_index("c")
    here = lax.axis_index("x")
    cuts = []
    for k in reversed(range(fan_x)):
        to = lax.rem(here + k, fan_x)
        for y in range(fan_y):
            for other in range(2):
                core = 1 - mine if other else mine
                at = pl.multiple_of(((to * fan_y + y) * 2 + core) * width, width)
                cuts.append(
                    pltpu.make_async_copy(
                        w_ref.at[:, pl.ds(at, width)],
                        outs[k].at[pl.ds(other * feats, feats), pl.ds(y * width, width)],
                        out_sem.at[(k * fan_y + y) * 2 + other],
                    )
                )
    for c in cuts:
        c.start()
    for i in range(shards):
        begin = seg_ref[i * rows]
        end = seg_ref[i * rows + rows - 1]
        whole = jnp.where(begin == end, 1.0, 0.0).astype(F32)
        marks_ref[pl.ds(i, 1), :] = jnp.full((1, LANES), whole, F32)
        if i + 1 < shards:
            on = jnp.where(end == seg_ref[(i + 1) * rows], 1.0, 0.0).astype(F32)
        else:
            on = jnp.float32(0.0)
        marks_ref[pl.ds(shards + i, 1), :] = jnp.full((1, LANES), on, F32)
    start = lax.axis_index("z") * rows
    last = seg_ref[start + rows - 1]

    def halve(_, span):
        low, high = span
        mid = (low + high) // 2
        inside = seg_ref[start + mid] == last
        return jnp.where(inside, low, mid + 1), jnp.where(inside, mid, high)

    first, _ = lax.fori_loop(0, rows.bit_length(), halve, (jnp.int32(0), jnp.int32(rows - 1)))
    first_ref[...] = jnp.full((SUB, LANES), first, jnp.int32)
    for c in cuts:
        c.wait()


def row(ref, at):
    return ref[pl.ds(at, SUB, stride=0), :]


def chain(ends_ref, marks_ref, rate, rows, visit):
    shards = ends_ref.shape[0]
    leap = jnp.exp(-float(rows) * rate)
    state = jnp.zeros(leap.shape, F32)
    modes = leap.shape[0]
    for i in range(shards - 1, -1, -1):
        visit(i, state)
        if i:
            whole = marks_ref[pl.ds(i, 1), :]
            on = marks_ref[pl.ds(shards + i - 1, 1), :]
            state = on * (ends_ref[i, :modes].astype(F32) + whole * (leap * state))


def taps_kernel(rows, ends_ref, marks_ref, rate_ref, out_ref):
    modes = rate_ref.shape[0]
    total = [jnp.zeros(rate_ref.shape, F32)]

    def visit(i, state):
        own = ends_ref[i, modes : 2 * modes].astype(F32)
        gain = ends_ref[i, 2 * modes :].astype(F32)
        total[0] = total[0] + (own + gain * state)

    chain(ends_ref, marks_ref, rate_ref[...], rows, visit)
    out_ref[...] = total[0]


def finish_kernel(
    ends_ref, marks_ref, res_ref, rate_ref, base_ref, first_ref, pay_ref, amp_v, pay_v, pay_sem
):
    rows = base_ref.shape[0]
    modes = res_ref.shape[0]
    me = lax.axis_index("z")
    own = [jnp.zeros(rate_ref.shape, F32)]

    def visit(i, state):
        own[0] = jnp.where(me == i, state, own[0])

    chain(ends_ref, marks_ref, rate_ref[...], rows, visit)
    amp_v[...] = own[0] * res_ref[...]
    first = first_ref[...]
    place = lax.broadcasted_iota(jnp.int32, (SUB, LANES), 0)
    back = (SUB - place).astype(F32)
    steps, terms = [], []
    for m in range(modes):
        rate = row(rate_ref, m)
        steps.append(jnp.exp(rate * -float(SUB)))
        terms.append(row(amp_v, m) * jnp.exp(rate * -back))

    def tokens(i, terms):
        terms = list(terms)
        at = pl.multiple_of(rows - 16 * (i + 1), 16)
        halves = []
        for h in (1, 0):
            tree = list(terms)
            while len(tree) > 1:
                tree = [tree[k] + tree[k + 1] for k in range(0, len(tree), 2)]
            halves.append(jnp.where(place + (at + SUB * h) >= first, tree[0], 0.0))
            terms = [a * b for a, b in zip(terms, steps)]
        carry = jnp.concatenate([halves[1], halves[0]], axis=0)
        pay_v[pl.ds(at, 16), :] = (base_ref[pl.ds(at, 16), :] + carry).astype(BF16)
        return tuple(terms)

    lax.fori_loop(0, rows // 16, tokens, tuple(terms))
    pays = [
        pltpu.make_async_copy(pay_v, pay_ref.at[i], pay_sem.at[i]) for i in range(pay_ref.shape[0])
    ]
    for c in pays:
        c.start()
    for c in pays:
        c.wait()


def product_kernel(fan_x, pay_ref, own_ref, got_ref, out_ref, conv):
    mine = lax.axis_index("c")
    here = lax.axis_index("x")
    for y in range(pay_ref.shape[0]):
        conv[:, y * LANES : (y + 1) * LANES] = pay_ref[y]
    for core, w_ref in ((mine, own_ref), (1 - mine, got_ref)):
        for k in range(0, fan_x, 2):
            pair = lax.dot_general(
                conv[...], w_ref[k * LANES : (k + 2) * LANES, :],
                (((1,), (1,)), ((), ())), preferred_element_type=F32,
            )
            for n in range(2):
                to = 2 * lax.rem(here + fan_x - k - n, fan_x) + core
                out_ref[to] = pair[:, n * LANES : (n + 1) * LANES].astype(BF16)


def sum_kernel(parts_ref, out_ref):
    total = parts_ref[0].astype(F32)
    for i in range(1, parts_ref.shape[0]):
        total = total + parts_ref[i].astype(F32)
    out_ref[...] = total.astype(BF16)


def cost(flops, nbytes):
    return pl.CostEstimate(flops=flops, bytes_accessed=nbytes, transcendentals=0)


def device(out_grad, conv_input, residues, decay_rate, segments, w_in):
    shards, fan_x, fan_y = (lax.axis_size(n) for n in ("z", "x", "y"))
    rows, chans = out_grad.shape
    modes = residues.shape[0]
    feats, depth = w_in.shape[0], w_in.shape[1] // (2 * fan_x)
    sem = pltpu.SemaphoreType.DMA
    whole = pltpu.CompilerParams(vmem_limit_bytes=67_000_000)
    small = pltpu.CompilerParams(vmem_limit_bytes=16 * 2**20)
    ends, base = pl.pallas_call(
        lambda *refs: scan_kernel(shards, *refs),
        name="scan",
        out_shape=(
            jax.ShapeDtypeStruct((shards, 3 * modes, chans), BF16),
            jax.ShapeDtypeStruct((rows, chans), F32),
        ),
        in_specs=[SM, VM, VM, VM, VM],
        out_specs=(HB, VM),
        scratch_shapes=[
            pltpu.VMEM((rows, chans), F32), pltpu.VMEM((rows, chans), F32),
            pltpu.VMEM((rows * SUB, chans), F32), pltpu.VMEM((3 * modes, chans), BF16),
            sem((shards,)),
        ],
        compiler_params=whole,
        cost_estimate=cost(10_000_000, 8_000_000),
    )(segments, out_grad, conv_input, residues, decay_rate)

    ends_in = lax.all_to_all(ends, "z", 0, 0)
    *cuts, marks, first = pl.pallas_call(
        lambda *refs: sort_kernel(shards, rows, fan_x, fan_y, *refs),
        name="sort",
        out_shape=(
            *(jax.ShapeDtypeStruct((2 * feats, depth), BF16) for _ in range(fan_x)),
            jax.ShapeDtypeStruct((2 * shards, chans), F32),
            jax.ShapeDtypeStruct((SUB, chans), jnp.int32),
        ),
        in_specs=[SM, pl.BlockSpec(memory_space=pltpu.HBM)],
        out_specs=(VM,) * (fan_x + 2),
        scratch_shapes=[sem((2 * fan_x * fan_y,))],
        compiler_params=small,
        cost_estimate=cost(100_000, 4_000_000),
    )(segments, w_in)
    for k in (1, 3, 2):
        cuts[k] = lax.ppermute(cuts[k], "x", [(i, (i + k) % fan_x) for i in range(fan_x)])
    pay = pl.pallas_call(
        finish_kernel,
        name="finish",
        out_shape=jax.ShapeDtypeStruct((fan_y, rows, chans), BF16),
        in_specs=[VM] * 6, out_specs=HB,
        scratch_shapes=[
            pltpu.VMEM((modes, chans), F32), pltpu.VMEM((rows, chans), BF16), sem((fan_y,)),
        ],
        compiler_params=small,
        cost_estimate=cost(10_000_000, 1_000_000),
    )(ends_in, marks, residues, decay_rate, base, first)
    pay_in = lax.all_to_all(pay, "y", 0, 0)
    own = jnp.concatenate([a[:feats] for a in cuts], axis=0)
    give = jnp.concatenate([a[feats:] for a in cuts], axis=0)
    got = lax.ppermute(give, "c", [(0, 1), (1, 0)])
    split = pl.pallas_call(
        lambda *refs: product_kernel(fan_x, *refs),
        name="product",
        out_shape=jax.ShapeDtypeStruct((2 * fan_x, rows, feats), BF16),
        in_specs=[VM] * 3, out_specs=VM,
        scratch_shapes=[pltpu.VMEM((rows, depth), BF16)],
        compiler_params=small,
        cost_estimate=cost(4 * rows * depth * fan_x * feats, 4_000_000),
    )(pay_in, own, got)
    split_in = lax.all_to_all(split, ("x", "c"), 0, 0)
    taps = pl.pallas_call(
        lambda *refs: taps_kernel(rows, *refs),
        name="taps",
        out_shape=jax.ShapeDtypeStruct((modes, chans), F32),
        in_specs=[VM] * 3, out_specs=VM,
        compiler_params=small,
        cost_estimate=cost(1_000_000, 300_000),
    )(ends_in, marks, decay_rate)
    d_input = pl.pallas_call(
        sum_kernel,
        name="total",
        out_shape=jax.ShapeDtypeStruct((rows, feats), BF16),
        in_specs=[VM], out_specs=VM,
        compiler_params=small,
        cost_estimate=cost(1_000_000, 900_000),
    )(split_in)
    return d_input, taps


def solution(mesh):
    grid = (16, 4, 8, 2)
    fine = Mesh(mesh.devices.reshape(grid), ("z", "x", "y", "c"))
    head = ("x", "y", "c")
    return jax.shard_map(
        device,
        mesh=fine,
        in_specs=(P("z", head), P("z", head), P(None, head), P(None, head), P(), P(head, None)),
        out_specs=(P("z", head), P(None, head)),
        check_vma=False,
    )
```

time: 127 us -> 104 us (0.82)
  the two profiles are of different devices: /device:TPU:10 before, /device:TPU:1 now
where the time goes in v2:
time: 104 us; the launch traced here: 102 us
  starting transfers between devices  53.7 us (52%)
  waiting for transfers between devices  26.8 us (26%)
  Pallas kernels  12.5 us (12%)
  local copies, waits for them, and re-layouts  8.56 us (8%)
    all_to_all x1, starting transfers between devices, device(): ends_in = lax.all_to_all(ends, 'z', 0, 0)  18.7 us
    all_to_all x1, waiting for transfers between devices, device(): split_in = lax.all_to_all(split, ('x', 'c'), 0, 0)  11.5 us
    ppermute x3, starting transfers between devices, device(): lax.ppermute(cuts[k], 'x', [(i, (i + k) % fan_x) for i in range(fan_x)])  11.5 us
    all_to_all x1, starting transfers between devices, device(): split_in = lax.all_to_all(split, ('x', 'c'), 0, 0)  9.36 us
    all_to_all x1, waiting for transfers between devices, device(): pay_in = lax.all_to_all(pay, 'y', 0, 0)  8.5 us
    ppermute x1, starting transfers between devices, device(): got = lax.ppermute(give, 'c', [(0, 1), (1, 0)])  7.29 us
    all_to_all x1, starting transfers between devices, device(): pay_in = lax.all_to_all(pay, 'y', 0, 0)  6.83 us
    slice x4, local copies, waits for them, and re-layouts, device(): give = jnp.concatenate([a[feats:] for a in cuts], axis=0)  4.62 us
  transfers between devices with their start and end apart: 7, of which 4 were waited for; matrix products, arithmetic and copies ran while one was open for 5% of the time, Pallas kernels for 6%

profile of v2, /device:TPU:1, one launch (start us, length us, event | category | flops | bytes accessed | tf_op | source)
XLA Modules:
  0.0 102.4 jit_solution(12200828058707508008)
XLA Ops:
  0.6 1.6 %copy-done = bf16[128,8192]{1,0:T(8,128)(2,1)S(1)} copy-done((bf16[128,8192]{1,0:T(8,128)(2,1)S(1)}, bf16[128,8192]{1,0:T(8,128)(2,1)}, u32[]{:S(2)}) %copy-start) | copy-done | bytes 2097176
  2.2 0.7 copy-done.3
  3.0 3.7 %sort.1 = (bf16[256,1024]{1,0:T(8,128)(2,1)S(1)}, bf16[256,1024]{1,0:T(8,128)(2,1)}, bf16[256,1024]{1,0:T(8,128)(2,1)}, bf16[256,1024]{1,0:T(8,128)(2,1)S(1)}, f...) custom-call(s32[6144]{0:T(1024)S(1)} %copy-done.3, bf16[128,8192]{1,0:T(8,128)(2,1)S(1)} %copy-done), custom_call_target="tpu_custom_call" | custom-call | flops 100000 | bytes 4000000 | tf_op jit(solution)/shard_map/sort/pallas_call | solution.py:253
  6.6 0.8 copy-done.1
  7.4 0.8 copy-done.6
  8.2 4.1 %collective-permute-start = (bf16[256,1024]{1,0:T(8,128)(2,1)}, bf16[256,1024]{1,0:T(8,128)(2,1)}, u32[]{:S(2)}, u32[]{:S(2)}) collective-permute-start(bf16[256,1024]{1,0:T(8,128)(2,1)} %get-tuple-element.15), channel_id=1, source_target_pairs={{0,16},{16,32},{32,48},{48,0},{1,17},{17,33},{33,49},{49,1},{2,18}... | collective-permute-start | bytes 1572872 | tf_op jit(solution)/shard_map/ppermute | solution.py:268
  12.3 4.4 %collective-permute-start.1 = (bf16[256,1024]{1,0:T(8,128)(2,1)}, bf16[256,1024]{1,0:T(8,128)(2,1)}, u32[]{:S(2)}, u32[]{:S(2)}) collective-permute-start(bf16[256,1024]{1,0:T(8,128)(2,1)} %get-tuple-element.16), channel_id=1, source_target_pairs={{0,32},{16,48},{32,0},{48,16},{1,33},{17,49},{33,1},{49,17},{2,34}... | collective-permute-start | bytes 1572872 | tf_op jit(solution)/shard_map/ppermute | solution.py:268
  16.7 4.0 %scan.1 = (bf16[16,48,128]{2,1,0:T(8,128)(2,1)}, f32[384,128]{1,0:T(8,128)}) custom-call(s32[6144]{0:T(1024)} %refs_0_.3, bf16[384,128]{1,0:T(8,128)(2,1)} %refs_1_.2, bf16[384,128]{1,0:T(8,128)(2,1)} %refs_2_.2, f32[16,128]{1,0:T(8,128)} %res_ref.1, f32[16,128]{1,0:T(8,128)} %refs_2_.3), custom_call_target="tpu_custom_call" | custom-call | flops 10000000 | bytes 8000000 | tf_op jit(solution)/shard_map/scan/pallas_call | solution.py:234
  20.7 18.7 %all-to-all-start = ((bf16[16,48,128]{2,1,0:T(8,128)(2,1)}), bf16[16,48,128]{2,1,0:T(8,128)(2,1)S(1)}, u32[]{:S(2)}, u32[]{:S(2)}) async-start(bf16[16,48,128]{2,1,0:T(8,128)(2,1)} %get-tuple-element.10), calls=%async_computation | async-start | bytes 393216 | tf_op jit(solution)/shard_map/all_to_all | solution.py:252
  39.4 3.1 %collective-permute-start.2 = (bf16[256,1024]{1,0:T(8,128)(2,1)}, bf16[256,1024]{1,0:T(8,128)(2,1)S(1)}, u32[]{:S(2)}, u32[]{:S(2)}) collective-permute-start(bf16[256,1024]{1,0:T(8,128)(2,1)} %copy-done.6), channel_id=1, source_target_pairs={{0,48},{16,0},{32,16},{48,32},{1,49},{17,1},{33,17},{49,33},{2,50}... | collective-permute-start | bytes 1572872 | tf_op jit(solution)/shard_map/ppermute | solution.py:268
  42.5 1.1 %fusion = (bf16[128,1024]{1,0:T(8,128)(2,1)S(1)}, bf16[128,1024]{1,0:T(8,128)(2,1)S(1)}) fusion(bf16[256,1024]{1,0:T(8,128)(2,1)} %copy-done.1), kind=kLoop, calls=%fused_computation.2 | loop fusion | bytes 1048576 | tf_op jit(solution)/shard_map/slice | solution.py:282
  43.6 1.8 %fusion.1 = (bf16[128,1024]{1,0:T(8,128)(2,1)S(1)}, bf16[128,1024]{1,0:T(8,128)(2,1)}) fusion(bf16[256,1024]{1,0:T(8,128)(2,1)} %collective-permute-done), kind=kLoop, calls=%fused_computation.3 | loop fusion | bytes 1048576 | tf_op jit(solution)/shard_map/slice | solution.py:282
  45.4 1.8 %fusion.2 = (bf16[128,1024]{1,0:T(8,128)(2,1)S(1)}, bf16[128,1024]{1,0:T(8,128)(2,1)}) fusion(bf16[256,1024]{1,0:T(8,128)(2,1)} %collective-permute-done.1), kind=kLoop, calls=%fused_computation.4 | loop fusion | bytes 1048576 | tf_op jit(solution)/shard_map/slice | solution.py:282
  47.1 4.6 %all-to-all-done.ends_ref.refs_0_ = bf16[16,48,128]{2,1,0:T(8,128)(2,1)S(1)} async-done(((bf16[16,48,128]{2,1,0:T(8,128)(2,1)}), bf16[16,48,128]{2,1,0:T(8,128)(2,1)S(1)}, u32[]{:S(2)}, u32[]{:S(2)}) %all-to-all-start) | async-done | bytes 196640 | tf_op jit(solution)/shard_map/all_to_all | solution.py:252
  51.8 1.4 %finish.1 = bf16[8,384,128]{2,1,0:T(8,128)(2,1)} custom-call(bf16[16,48,128]{2,1,0:T(8,128)(2,1)S(1)} %all-to-all-done.ends_ref.refs_0_, f32[32,128]{1,0:T(8,128)S(1)} %get-tuple-element.11.marks_ref.refs_1_, f32[16,128]{1,0:T(8,128)S(1)} %copy-done.5, f32[16,128]{1,0:T(8,128)S(1)} %copy-done.4, f32[384,128]{1,0:T(8,128)S(1)} %copy-done.2, ...), custom_call_target="tpu_custom_call" | custom-call | flops 10000000 | bytes 1000000 | tf_op jit(solution)/shard_map/finish/pallas_call | solution.py:269
  53.1 6.8 %all-to-all-start.1 = ((bf16[8,384,128]{2,1,0:T(8,128)(2,1)}), bf16[8,384,128]{2,1,0:T(8,128)(2,1)S(1)}, u32[]{:S(2)}, u32[]{:S(2)}) async-start(bf16[8,384,128]{2,1,0:T(8,128)(2,1)} %finish.1), calls=%async_computation.1 | async-start | bytes 1572864 | tf_op jit(solution)/shard_map/all_to_all | solution.py:280
  60.1 7.3 %collective-permute-start.3 = (bf16[512,1024]{1,0:T(8,128)(2,1)S(1)}, bf16[512,1024]{1,0:T(8,128)(2,1)S(1)}, u32[]{:S(2)}, u32[]{:S(2)}) collective-permute-start(bf16[512,1024]{1,0:T(8,128)(2,1)S(1)} %pad_maximum_fusion.1), channel_id=1, source_target_pairs={{0,1},{1,0},{2,3},{3,2},{4,5},{5,4},{6,7},{7,6},{8,9},{9,8},{10,11... | collective-permute-start | bytes 3145736 | tf_op jit(solution)/shard_map/ppermute | solution.py:283
  67.5 2.2 %collective-permute-done.3.refs_2_ = bf16[512,1024]{1,0:T(8,128)(2,1)S(1)} collective-permute-done((bf16[512,1024]{1,0:T(8,128)(2,1)S(1)}, bf16[512,1024]{1,0:T(8,128)(2,1)S(1)}, u32[]{:S(2)}, u32[]{:S(2)}) %collective-permute-start.3) | collective-permute-done | bytes 1048608 | tf_op jit(solution)/shard_map/ppermute | solution.py:283
  69.7 8.5 %all-to-all-done.1.refs_0_ = bf16[8,384,128]{2,1,0:T(8,128)(2,1)S(1)} async-done(((bf16[8,384,128]{2,1,0:T(8,128)(2,1)}), bf16[8,384,128]{2,1,0:T(8,128)(2,1)S(1)}, u32[]{:S(2)}, u32[]{:S(2)}) %all-to-all-start.1) | async-done | bytes 786464 | tf_op jit(solution)/shard_map/all_to_all | solution.py:280
  78.2 2.0 %product.1 = bf16[8,384,128]{2,1,0:T(8,128)(2,1)} custom-call(bf16[8,384,128]{2,1,0:T(8,128)(2,1)S(1)} %all-to-all-done.1.refs_0_, bf16[512,1024]{1,0:T(8,128)(2,1)S(1)} %pad_maximum_fusion.refs_1_, bf16[512,1024]{1,0:T(8,128)(2,1)S(1)} %collective-permute-done.3.refs_2_), custom_call_target="tpu_custom_call" | custom-call | flops 805306368 | bytes 4000000 | tf_op jit(solution)/shard_map/product/pallas_call | solution.py:284
  80.1 9.4 %all-to-all-start.2 = ((bf16[8,384,128]{2,1,0:T(8,128)(2,1)}), bf16[8,384,128]{2,1,0:T(8,128)(2,1)S(1)}, u32[]{:S(2)}, u32[]{:S(2)}) async-start(bf16[8,384,128]{2,1,0:T(8,128)(2,1)} %product.1), calls=%async_computation.2 | async-start | bytes 1572864 | tf_op jit(solution)/shard_map/all_to_all | solution.py:293
  89.5 0.7 taps.1
  90.2 11.5 %all-to-all-done.2.parts_ref = bf16[8,384,128]{2,1,0:T(8,128)(2,1)S(1)} async-done(((bf16[8,384,128]{2,1,0:T(8,128)(2,1)}), bf16[8,384,128]{2,1,0:T(8,128)(2,1)S(1)}, u32[]{:S(2)}, u32[]{:S(2)}) %all-to-all-start.2) | async-done | bytes 786464 | tf_op jit(solution)/shard_map/all_to_all | solution.py:293
  101.7 0.7 total.1
  (20 shorter events, 0.2 us)
Async XLA Ops:
  0.6 1.6 %copy-start = (bf16[128,8192]{1,0:T(8,128)(2,1)S(1)}, bf16[128,8192]{1,0:T(8,128)(2,1)}, u32[]{:S(2)}) copy-start(bf16[128,8192]{1,0:T(8,128)(2,1)} %refs_1_.3) | copy-start | bytes 6291460
  2.2 0.7 copy-start.3
  6.6 0.8 copy-start.1
  7.4 0.8 copy-start.6
  8.2 43.5 %copy-start.4 = (f32[16,128]{1,0:T(8,128)S(1)}, f32[16,128]{1,0:T(8,128)}, u32[]{:S(2)}) copy-start(f32[16,128]{1,0:T(8,128)} %refs_2_.3) | copy-start | bytes 24580
  8.2 43.5 %copy-start.5 = (f32[16,128]{1,0:T(8,128)S(1)}, f32[16,128]{1,0:T(8,128)}, u32[]{:S(2)}) copy-start(f32[16,128]{1,0:T(8,128)} %res_ref.1) | copy-start | bytes 24580
  8.2 35.4 %collective-permute-start = (bf16[256,1024]{1,0:T(8,128)(2,1)}, bf16[256,1024]{1,0:T(8,128)(2,1)}, u32[]{:S(2)}, u32[]{:S(2)}) collective-permute-start(bf16[256,1024]{1,0:T(8,128)(2,1)} %get-tuple-element.15), channel_id=1, source_target_pairs={{0,16},{16,32},{32,48},{48,0},{1,17},{17,33},{33,49},{49,1},{2,18}... | collective-permute-start | bytes 1572872 | tf_op jit(solution)/shard_map/ppermute | solution.py:268
  12.3 33.1 %collective-permute-start.1 = (bf16[256,1024]{1,0:T(8,128)(2,1)}, bf16[256,1024]{1,0:T(8,128)(2,1)}, u32[]{:S(2)}, u32[]{:S(2)}) collective-permute-start(bf16[256,1024]{1,0:T(8,128)(2,1)} %get-tuple-element.16), channel_id=1, source_target_pairs={{0,32},{16,48},{32,0},{48,16},{1,33},{17,49},{33,1},{49,17},{2,34}... | collective-permute-start | bytes 1572872 | tf_op jit(solution)/shard_map/ppermute | solution.py:268
  20.7 31.0 %copy-start.2 = (f32[384,128]{1,0:T(8,128)S(1)}, f32[384,128]{1,0:T(8,128)}, u32[]{:S(2)}) copy-start(f32[384,128]{1,0:T(8,128)} %get-tuple-element.12.base_ref) | copy-start | bytes 589828
  20.7 31.0 %all-to-all-start = ((bf16[16,48,128]{2,1,0:T(8,128)(2,1)}), bf16[16,48,128]{2,1,0:T(8,128)(2,1)S(1)}, u32[]{:S(2)}, u32[]{:S(2)}) async-start(bf16[16,48,128]{2,1,0:T(8,128)(2,1)} %get-tuple-element.10), calls=%async_computation | async-start | bytes 393216 | tf_op jit(solution)/shard_map/all_to_all | solution.py:252
  39.4 20.5 %collective-permute-start.2 = (bf16[256,1024]{1,0:T(8,128)(2,1)}, bf16[256,1024]{1,0:T(8,128)(2,1)S(1)}, u32[]{:S(2)}, u32[]{:S(2)}) collective-permute-start(bf16[256,1024]{1,0:T(8,128)(2,1)} %copy-done.6), channel_id=1, source_target_pairs={{0,48},{16,0},{32,16},{48,32},{1,49},{17,1},{33,17},{49,33},{2,50}... | collective-permute-start | bytes 1572872 | tf_op jit(solution)/shard_map/ppermute | solution.py:268
  53.1 25.1 %all-to-all-start.1 = ((bf16[8,384,128]{2,1,0:T(8,128)(2,1)}), bf16[8,384,128]{2,1,0:T(8,128)(2,1)S(1)}, u32[]{:S(2)}, u32[]{:S(2)}) async-start(bf16[8,384,128]{2,1,0:T(8,128)(2,1)} %finish.1), calls=%async_computation.1 | async-start | bytes 1572864 | tf_op jit(solution)/shard_map/all_to_all | solution.py:280
  60.0 7.5 %copy-start.7 = (bf16[128,1024]{1,0:T(8,128)(2,1)S(1)}, bf16[128,1024]{1,0:T(8,128)(2,1)}, u32[]{:S(2)}) copy-start(bf16[128,1024]{1,0:T(8,128)(2,1)} %get-tuple-element.21) | copy-start | bytes 786436
  60.0 7.5 %copy-start.8 = (bf16[128,1024]{1,0:T(8,128)(2,1)S(1)}, bf16[128,1024]{1,0:T(8,128)(2,1)}, u32[]{:S(2)}) copy-start(bf16[128,1024]{1,0:T(8,128)(2,1)} %get-tuple-element.23) | copy-start | bytes 786436
  60.1 9.6 %collective-permute-start.3 = (bf16[512,1024]{1,0:T(8,128)(2,1)S(1)}, bf16[512,1024]{1,0:T(8,128)(2,1)S(1)}, u32[]{:S(2)}, u32[]{:S(2)}) collective-permute-start(bf16[512,1024]{1,0:T(8,128)(2,1)S(1)} %pad_maximum_fusion.1), channel_id=1, source_target_pairs={{0,1},{1,0},{2,3},{3,2},{4,5},{5,4},{6,7},{7,6},{8,9},{9,8},{10,11... | collective-permute-start | bytes 3145736 | tf_op jit(solution)/shard_map/ppermute | solution.py:283
  80.1 21.5 %all-to-all-start.2 = ((bf16[8,384,128]{2,1,0:T(8,128)(2,1)}), bf16[8,384,128]{2,1,0:T(8,128)(2,1)S(1)}, u32[]{:S(2)}, u32[]{:S(2)}) async-start(bf16[8,384,128]{2,1,0:T(8,128)(2,1)} %product.1), calls=%async_computation.2 | async-start | bytes 1572864 | tf_op jit(solution)/shard_map/all_to_all | solution.py:293

commit v3 on v2

--- a/solution.py
+++ b/solution.py
@@ -17,11 +17,14 @@
 
 
 def scan_kernel(
-    shards, seg_ref, g_ref, x_ref, res_ref, rate_ref,
-    ends_ref, base_ref, gf, xf, prod, end_v, end_sem,
+    shards, fan_x, fan_y, seg_ref, g_ref, x_ref, res_ref, rate_ref, w_ref,
+    ends_ref, base_ref, *refs
 ):
+    outs, (gf, xf, prod, end_v, w_v, w_sem, cut_sem, end_sem) = refs[:fan_x], refs[fan_x:]
     rows = g_ref.shape[0]
     base = lax.axis_index("z") * rows
+    w_in = pltpu.make_async_copy(w_ref, w_v, w_sem)
+    w_in.start()
     gf[...] = g_ref[...].astype(F32)
     xf[...] = x_ref[...].astype(F32)
     decay = jnp.exp(-rate_ref[...])
@@ -53,9 +56,35 @@
         return a0, a1, f0, f1, g0, g1, c0, c1, nxt
 
     init = (zero, zero, zero, zero, one, one, zero, zero, seg_ref[base + rows - 1])
-    a0, a1, f0, f1, _, _, c0, c1, _ = lax.fori_loop(0, rows // 16, block, init)
-    for n, pair in enumerate(((a0, a1), (f0, f1), (c0, c1))):
-        end_v[16 * n : 16 * n + 16] = jnp.concatenate(pair, axis=0).astype(BF16)
+    half = lax.fori_loop(0, rows // 32, block, init)
+    w_in.wait()
+    feats = w_v.shape[0]
+    width = w_v.shape[1] // (2 * fan_x * fan_y)
+    mine = lax.axis_index("c")
+    here = lax.axis_index("x")
+    cuts = []
+    for k in range(fan_x):
+        to = lax.rem(here + k, fan_x)
+        for y in range(fan_y):
+            for other in range(2):
+                core = 1 - mine if other else mine
+                at = pl.multiple_of(((to * fan_y + y) * 2 + core) * width, width)
+                cuts.append(
+                    pltpu.make_async_copy(
+                        w_v.at[:, pl.ds(at, width)],
+                        outs[k].at[pl.ds(other * feats, feats), pl.ds(y * width, width)],
+                        cut_sem.at[(k * fan_y + y) * 2 + other],
+                    )
+                )
+    for c in cuts:
+        c.start()
+    a0, a1, f0, f1, _, _, c0, c1, _ = lax.fori_loop(rows // 32, rows // 16, block, half)
+    state = jnp.concatenate((a0, a1), axis=0)
+    high = state.astype(BF16)
+    end_v[:16] = high
+    end_v[16:32] = (state - high.astype(F32)).astype(BF16)
+    end_v[32:48] = jnp.concatenate((f0, f1), axis=0).astype(BF16)
+    end_v[48:] = jnp.concatenate((c0, c1), axis=0).astype(BF16)
     ends = [pltpu.make_async_copy(end_v, ends_ref.at[i], end_sem.at[i]) for i in range(shards)]
     for c in ends:
         c.start()
@@ -69,32 +98,12 @@
         return 0
 
     lax.fori_loop(0, rows // 16, fold, 0)
-    for c in ends:
+    for c in cuts + ends:
         c.wait()
 
 
-def sort_kernel(shards, rows, fan_x, fan_y, seg_ref, w_ref, *refs):
-    outs, (marks_ref, first_ref, out_sem) = refs[:fan_x], refs[fan_x:]
-    feats = w_ref.shape[0]
-    width = w_ref.shape[1] // (2 * fan_x * fan_y)
-    mine = lax.axis_index("c")
-    here = lax.axis_index("x")
-    cuts = []
-    for k in reversed(range(fan_x)):
-        to = lax.rem(here + k, fan_x)
-        for y in range(fan_y):
-            for other in range(2):
-                core = 1 - mine if other else mine
-                at = pl.multiple_of(((to * fan_y + y) * 2 + core) * width, width)
-                cuts.append(
-                    pltpu.make_async_copy(
-                        w_ref.at[:, pl.ds(at, width)],
-                        outs[k].at[pl.ds(other * feats, feats), pl.ds(y * width, width)],
-                        out_sem.at[(k * fan_y + y) * 2 + other],
-                    )
-                )
-    for c in cuts:
-        c.start()
+def marks_kernel(shards, rows, seg_ref, base_ref, marks_ref, first_ref, same_ref):
+    same_ref[...] = base_ref[...]
     for i in range(shards):
         begin = seg_ref[i * rows]
         end = seg_ref[i * rows + rows - 1]
@@ -116,8 +125,6 @@
 
     first, _ = lax.fori_loop(0, rows.bit_length(), halve, (jnp.int32(0), jnp.int32(rows - 1)))
     first_ref[...] = jnp.full((SUB, LANES), first, jnp.int32)
-    for c in cuts:
-        c.wait()
 
 
 def row(ref, at):
@@ -134,7 +141,8 @@
         if i:
             whole = marks_ref[pl.ds(i, 1), :]
             on = marks_ref[pl.ds(shards + i - 1, 1), :]
-            state = on * (ends_ref[i, :modes].astype(F32) + whole * (leap * state))
+            head = ends_ref[i, :modes].astype(F32) + ends_ref[i, modes : 2 * modes].astype(F32)
+            state = on * (head + whole * (leap * state))
 
 
 def taps_kernel(rows, ends_ref, marks_ref, rate_ref, out_ref):
@@ -142,8 +150,8 @@
     total = [jnp.zeros(rate_ref.shape, F32)]
 
     def visit(i, state):
-        own = ends_ref[i, modes : 2 * modes].astype(F32)
-        gain = ends_ref[i, 2 * modes :].astype(F32)
+        own = ends_ref[i, 2 * modes : 3 * modes].astype(F32)
+        gain = ends_ref[i, 3 * modes :].astype(F32)
         total[0] = total[0] + (own + gain * state)
 
     chain(ends_ref, marks_ref, rate_ref[...], rows, visit)
@@ -231,39 +239,38 @@
     sem = pltpu.SemaphoreType.DMA
     whole = pltpu.CompilerParams(vmem_limit_bytes=67_000_000)
     small = pltpu.CompilerParams(vmem_limit_bytes=16 * 2**20)
-    ends, base = pl.pallas_call(
-        lambda *refs: scan_kernel(shards, *refs),
+    ends, base, *cuts = pl.pallas_call(
+        lambda *refs: scan_kernel(shards, fan_x, fan_y, *refs),
         name="scan",
         out_shape=(
-            jax.ShapeDtypeStruct((shards, 3 * modes, chans), BF16),
+            jax.ShapeDtypeStruct((shards, 4 * modes, chans), BF16),
             jax.ShapeDtypeStruct((rows, chans), F32),
+            *(jax.ShapeDtypeStruct((2 * feats, depth), BF16) for _ in range(fan_x)),
         ),
-        in_specs=[SM, VM, VM, VM, VM],
-        out_specs=(HB, VM),
+        in_specs=[SM, VM, VM, VM, VM, HB],
+        out_specs=(HB, VM, *(HB,) * fan_x),
         scratch_shapes=[
             pltpu.VMEM((rows, chans), F32), pltpu.VMEM((rows, chans), F32),
-            pltpu.VMEM((rows * SUB, chans), F32), pltpu.VMEM((3 * modes, chans), BF16),
-            sem((shards,)),
+            pltpu.VMEM((rows * SUB, chans), F32), pltpu.VMEM((4 * modes, chans), BF16),
+            pltpu.VMEM(w_in.shape, BF16), sem(()), sem((2 * fan_x * fan_y,)), sem((shards,)),
         ],
         compiler_params=whole,
         cost_estimate=cost(10_000_000, 8_000_000),
-    )(segments, out_grad, conv_input, residues, decay_rate)
+    )(segments, out_grad, conv_input, residues, decay_rate, w_in)
 
     ends_in = lax.all_to_all(ends, "z", 0, 0)
-    *cuts, marks, first = pl.pallas_call(
-        lambda *refs: sort_kernel(shards, rows, fan_x, fan_y, *refs),
-        name="sort",
+    marks, first, base = pl.pallas_call(
+        lambda *refs: marks_kernel(shards, rows, *refs),
+        name="marks",
         out_shape=(
-            *(jax.ShapeDtypeStruct((2 * feats, depth), BF16) for _ in range(fan_x)),
             jax.ShapeDtypeStruct((2 * shards, chans), F32),
             jax.ShapeDtypeStruct((SUB, chans), jnp.int32),
+            jax.ShapeDtypeStruct((rows, chans), F32),
         ),
-        in_specs=[SM, pl.BlockSpec(memory_space=pltpu.HBM)],
-        out_specs=(VM,) * (fan_x + 2),
-        scratch_shapes=[sem((2 * fan_x * fan_y,))],
-        compiler_params=small,
-        cost_estimate=cost(100_000, 4_000_000),
-    )(segments, w_in)
+        in_specs=[SM, VM], out_specs=(VM, VM, VM),
+        compiler_params=small,
+        cost_estimate=cost(100_000, 100_000),
+    )(segments, base)
     for k in (1, 3, 2):
         cuts[k] = lax.ppermute(cuts[k], "x", [(i, (i + k) % fan_x) for i in range(fan_x)])
     pay = pl.pallas_call(

time: 104 us -> 97.3 us (0.936)
  waiting for transfers between devices: 26.8 us -> 33 us
  starting transfers between devices: 53.7 us -> 47.7 us
  local copies, waits for them, and re-layouts: 8.56 us -> 3.5 us
    ppermute x3, waiting for transfers between devices: 0.01 us -> 6.62 us  [device(): lax.ppermute(cuts[k], 'x', [(i, (i + k) % fan_x) for i in range(fan_x)])]
    all_to_all x1, waiting for transfers between devices: 4.62 us -> 0.01 us  [device(): ends_in = lax.all_to_all(ends, 'z', 0, 0)]
    all_to_all x1, waiting for transfers between devices: 8.5 us -> 12.7 us  [device(): pay_in = lax.all_to_all(pay, 'y', 0, 0)]
    ppermute x1, starting transfers between devices: 7.29 us -> 3.36 us  [device(): got = lax.ppermute(give, 'c', [(0, 1), (1, 0)])]
    unnamed x18 -> x12, local copies, waits for them, and re-layouts: 3.94 us -> 0.94 us
    slice x4, local copies, waits for them, and re-layouts: 4.62 us -> 2.56 us  [device(): give = jnp.concatenate([a[feats:] for a in cuts], axis=0)]
    all_to_all x1, starting transfers between devices: 9.36 us -> 7.55 us  [device(): split_in = lax.all_to_all(split, ('x', 'c'), 0, 0)]
  transfers between devices with their start and end apart: 7 -> 7, of which waited for: 4 -> 5; matrix products, arithmetic and copies ran while one was open for 5% -> 3% of each run, Pallas kernels for 6% -> 3%
where the time goes in v3:
time: 97.3 us; the launch traced here: 96.7 us
  starting transfers between devices  47.7 us (49%)
  waiting for transfers between devices  33 us (34%)
  Pallas kernels  11.5 us (12%)
  local copies, waits for them, and re-layouts  3.5 us (4%)
    all_to_all x1, starting transfers between devices, device(): ends_in = lax.all_to_all(ends, 'z', 0, 0)  18.6 us
    all_to_all x1, waiting for transfers between devices, device(): pay_in = lax.all_to_all(pay, 'y', 0, 0)  12.7 us
    all_to_all x1, waiting for transfers between devices, device(): split_in = lax.all_to_all(split, ('x', 'c'), 0, 0)  11.5 us
    ppermute x3, starting transfers between devices, device(): lax.ppermute(cuts[k], 'x', [(i, (i + k) % fan_x) for i in range(fan_x)])  11.4 us
    all_to_all x1, starting transfers between devices, device(): split_in = lax.all_to_all(split, ('x', 'c'), 0, 0)  7.55 us
    all_to_all x1, starting transfers between devices, device(): pay_in = lax.all_to_all(pay, 'y', 0, 0)  6.83 us
    ppermute x3, waiting for transfers between devices, device(): lax.ppermute(cuts[k], 'x', [(i, (i + k) % fan_x) for i in range(fan_x)])  6.62 us
    pallas_call x1, Pallas kernels, device(): pl.pallas_call(lambda *refs: scan_kernel(shards, fan_x, fan_y, *refs), na...  5.68 us
  transfers between devices with their start and end apart: 7, of which 5 were waited for; matrix products, arithmetic and copies ran while one was open for 3% of the time, Pallas kernels for 3%

profile of v3, /device:TPU:1, one launch (start us, length us, event | category | flops | bytes accessed | tf_op | source)
XLA Modules:
  0.0 96.7 jit_solution(13258546895939547936)
XLA Ops:
  0.6 5.7 %scan.1 = (bf16[16,64,128]{2,1,0:T(8,128)(2,1)}, f32[384,128]{1,0:T(8,128)}, bf16[256,1024]{1,0:T(8,128)(2,1)}, bf16[256,1024]{1,0:T(8,128)(2,1)}, bf16[256,1024]{1,0:T(8,128)(2,1)}, /*index=5*/bf16[256,1024]{1,0:T(8,128)(2,1)}) custom-call(s32[6144]{0:T(1024)} %refs_0_.3, bf16[384,128]{1,0:T(8,128)(2,1)} %refs_1_.1, bf16[384,128]{1,0:T(8,128)(2,1)} %refs_2_.2, ...), custom_call_target="tpu_custom_call" | custom-call | flops 10000000 | bytes 8000000 | tf_op jit(solution)/shard_map/scan/pallas_call | solution.py:242
  6.3 3.9 %collective-permute-start = (bf16[256,1024]{1,0:T(8,128)(2,1)}, bf16[256,1024]{1,0:T(8,128)(2,1)S(1)}, u32[]{:S(2)}, u32[]{:S(2)}) collective-permute-start(bf16[256,1024]{1,0:T(8,128)(2,1)} %get-tuple-element.17), channel_id=1, source_target_pairs={{0,16},{16,32},{32,48},{48,0},{1,17},{17,33},{33,49},{49,1},{2,18}... | collective-permute-start | bytes 1572872 | tf_op jit(solution)/shard_map/ppermute | solution.py:275
  10.3 18.6 %all-to-all-start = ((bf16[16,64,128]{2,1,0:T(8,128)(2,1)}), bf16[16,64,128]{2,1,0:T(8,128)(2,1)S(1)}, u32[]{:S(2)}, u32[]{:S(2)}) async-start(bf16[16,64,128]{2,1,0:T(8,128)(2,1)} %get-tuple-element.11), calls=%async_computation | async-start | bytes 524288 | tf_op jit(solution)/shard_map/all_to_all | solution.py:261
  28.9 4.4 %collective-permute-start.1 = (bf16[256,1024]{1,0:T(8,128)(2,1)}, bf16[256,1024]{1,0:T(8,128)(2,1)S(1)}, u32[]{:S(2)}, u32[]{:S(2)}) collective-permute-start(bf16[256,1024]{1,0:T(8,128)(2,1)} %get-tuple-element.18), channel_id=1, source_target_pairs={{0,32},{16,48},{32,0},{48,16},{1,33},{17,49},{33,1},{49,17},{2,34}... | collective-permute-start | bytes 1572872 | tf_op jit(solution)/shard_map/ppermute | solution.py:275
  33.3 3.1 %collective-permute-start.2 = (bf16[256,1024]{1,0:T(8,128)(2,1)}, bf16[256,1024]{1,0:T(8,128)(2,1)S(1)}, u32[]{:S(2)}, u32[]{:S(2)}) collective-permute-start(bf16[256,1024]{1,0:T(8,128)(2,1)} %get-tuple-element.19), channel_id=1, source_target_pairs={{0,48},{16,0},{32,16},{48,32},{1,49},{17,1},{33,17},{49,33},{2,50}... | collective-permute-start | bytes 1572872 | tf_op jit(solution)/shard_map/ppermute | solution.py:275
  36.3 1.1 %fusion = (bf16[128,1024]{1,0:T(8,128)(2,1)S(1)}, bf16[128,1024]{1,0:T(8,128)(2,1)S(1)}) fusion(bf16[256,1024]{1,0:T(8,128)(2,1)} %get-tuple-element.16), kind=kLoop, calls=%fused_computation.2 | loop fusion | bytes 1048576 | tf_op jit(solution)/shard_map/slice | solution.py:289
  37.4 0.9 copy-done
  38.3 1.1 %marks.1 = (f32[32,128]{1,0:T(8,128)S(1)}, s32[8,128]{1,0:T(8,128)S(1)}, f32[384,128]{1,0:T(8,128)S(1)}) custom-call(s32[6144]{0:T(1024)S(1)} %copy-done.1, f32[384,128]{1,0:T(8,128)S(1)} %copy-done), custom_call_target="tpu_custom_call" | custom-call | flops 100000 | bytes 100000 | tf_op jit(solution)/shard_map/marks/pallas_call | solution.py:262
  39.5 0.7 fusion.1
  40.2 4.6 %collective-permute-done.1 = bf16[256,1024]{1,0:T(8,128)(2,1)S(1)} collective-permute-done((bf16[256,1024]{1,0:T(8,128)(2,1)}, bf16[256,1024]{1,0:T(8,128)(2,1)S(1)}, u32[]{:S(2)}, u32[]{:S(2)}) %collective-permute-start.1) | collective-permute-done | bytes 524320 | tf_op jit(solution)/shard_map/ppermute | solution.py:275
  44.8 0.7 fusion.2
  45.5 1.3 %finish.1 = bf16[8,384,128]{2,1,0:T(8,128)(2,1)} custom-call(bf16[16,64,128]{2,1,0:T(8,128)(2,1)S(1)} %all-to-all-done.ends_ref.refs_0_, f32[32,128]{1,0:T(8,128)S(1)} %get-tuple-element.13.marks_ref.refs_1_, f32[16,128]{1,0:T(8,128)S(1)} %copy-done.3, f32[16,128]{1,0:T(8,128)S(1)} %copy-done.2, f32[384,128]{1,0:T(8,128)S(1)} %get-tuple-element.14.base_ref, ...), custom_call_target="tpu_custom_call" | custom-call | flops 10000000 | bytes 1000000 | tf_op jit(solution)/shard_map/finish/pallas_call | solution.py:276
  46.8 6.8 %all-to-all-start.1 = ((bf16[8,384,128]{2,1,0:T(8,128)(2,1)}), bf16[8,384,128]{2,1,0:T(8,128)(2,1)S(1)}, u32[]{:S(2)}, u32[]{:S(2)}) async-start(bf16[8,384,128]{2,1,0:T(8,128)(2,1)} %finish.1), calls=%async_computation.1 | async-start | bytes 1572864 | tf_op jit(solution)/shard_map/all_to_all | solution.py:287
  53.7 2.1 %collective-permute-done.2 = bf16[256,1024]{1,0:T(8,128)(2,1)S(1)} collective-permute-done((bf16[256,1024]{1,0:T(8,128)(2,1)}, bf16[256,1024]{1,0:T(8,128)(2,1)S(1)}, u32[]{:S(2)}, u32[]{:S(2)}) %collective-permute-start.2) | collective-permute-done | bytes 524320 | tf_op jit(solution)/shard_map/ppermute | solution.py:275
  55.8 0.1 pad_maximum_fusion.1
  55.9 3.4 %collective-permute-start.3 = (bf16[512,1024]{1,0:T(8,128)(2,1)S(1)}, bf16[512,1024]{1,0:T(8,128)(2,1)S(1)}, u32[]{:S(2)}, u32[]{:S(2)}) collective-permute-start(bf16[512,1024]{1,0:T(8,128)(2,1)S(1)} %pad_maximum_fusion.1), channel_id=1, source_target_pairs={{0,1},{1,0},{2,3},{3,2},{4,5},{5,4},{6,7},{7,6},{8,9},{9,8},{10,11... | collective-permute-start | bytes 3145736 | tf_op jit(solution)/shard_map/ppermute | solution.py:290
  59.3 0.1 pad_maximum_fusion.refs_1_
  59.3 2.2 %collective-permute-done.3.refs_2_ = bf16[512,1024]{1,0:T(8,128)(2,1)S(1)} collective-permute-done((bf16[512,1024]{1,0:T(8,128)(2,1)S(1)}, bf16[512,1024]{1,0:T(8,128)(2,1)S(1)}, u32[]{:S(2)}, u32[]{:S(2)}) %collective-permute-start.3) | collective-permute-done | bytes 1048608 | tf_op jit(solution)/shard_map/ppermute | solution.py:290
  61.5 12.7 %all-to-all-done.1.refs_0_ = bf16[8,384,128]{2,1,0:T(8,128)(2,1)S(1)} async-done(((bf16[8,384,128]{2,1,0:T(8,128)(2,1)}), bf16[8,384,128]{2,1,0:T(8,128)(2,1)S(1)}, u32[]{:S(2)}, u32[]{:S(2)}) %all-to-all-start.1) | async-done | bytes 786464 | tf_op jit(solution)/shard_map/all_to_all | solution.py:287
  74.2 2.0 %product.1 = bf16[8,384,128]{2,1,0:T(8,128)(2,1)} custom-call(bf16[8,384,128]{2,1,0:T(8,128)(2,1)S(1)} %all-to-all-done.1.refs_0_, bf16[512,1024]{1,0:T(8,128)(2,1)S(1)} %pad_maximum_fusion.refs_1_, bf16[512,1024]{1,0:T(8,128)(2,1)S(1)} %collective-permute-done.3.refs_2_), custom_call_target="tpu_custom_call" | custom-call | flops 805306368 | bytes 4000000 | tf_op jit(solution)/shard_map/product/pallas_call | solution.py:291
  76.2 7.6 %all-to-all-start.2 = ((bf16[8,384,128]{2,1,0:T(8,128)(2,1)}), bf16[8,384,128]{2,1,0:T(8,128)(2,1)S(1)}, u32[]{:S(2)}, u32[]{:S(2)}) async-start(bf16[8,384,128]{2,1,0:T(8,128)(2,1)} %product.1), calls=%async_computation.2 | async-start | bytes 1572864 | tf_op jit(solution)/shard_map/all_to_all | solution.py:300
  83.8 0.7 taps.1
  84.4 11.5 %all-to-all-done.2.parts_ref = bf16[8,384,128]{2,1,0:T(8,128)(2,1)S(1)} async-done(((bf16[8,384,128]{2,1,0:T(8,128)(2,1)}), bf16[8,384,128]{2,1,0:T(8,128)(2,1)S(1)}, u32[]{:S(2)}, u32[]{:S(2)}) %all-to-all-start.2) | async-done | bytes 786464 | tf_op jit(solution)/shard_map/all_to_all | solution.py:300
  95.9 0.7 total.1
  (14 shorter events, 0.1 us)
Async XLA Ops:
  0.6 36.8 %copy-start.1 = (s32[6144]{0:T(1024)S(1)}, s32[6144]{0:T(1024)}, u32[]{:S(2)}) copy-start(s32[6144]{0:T(1024)} %refs_0_.3) | copy-start | bytes 73732
  6.3 39.2 %copy-start.2 = (f32[16,128]{1,0:T(8,128)S(1)}, f32[16,128]{1,0:T(8,128)}, u32[]{:S(2)}) copy-start(f32[16,128]{1,0:T(8,128)} %refs_2_.3) | copy-start | bytes 24580
  6.3 39.1 %copy-start.3 = (f32[16,128]{1,0:T(8,128)S(1)}, f32[16,128]{1,0:T(8,128)}, u32[]{:S(2)}) copy-start(f32[16,128]{1,0:T(8,128)} %res_ref.1) | copy-start | bytes 24580
  6.3 33.1 %collective-permute-start = (bf16[256,1024]{1,0:T(8,128)(2,1)}, bf16[256,1024]{1,0:T(8,128)(2,1)S(1)}, u32[]{:S(2)}, u32[]{:S(2)}) collective-permute-start(bf16[256,1024]{1,0:T(8,128)(2,1)} %get-tuple-element.17), channel_id=1, source_target_pairs={{0,16},{16,32},{32,48},{48,0},{1,17},{17,33},{33,49},{49,1},{2,18}... | collective-permute-start | bytes 1572872 | tf_op jit(solution)/shard_map/ppermute | solution.py:275
  10.3 35.2 %all-to-all-start = ((bf16[16,64,128]{2,1,0:T(8,128)(2,1)}), bf16[16,64,128]{2,1,0:T(8,128)(2,1)S(1)}, u32[]{:S(2)}, u32[]{:S(2)}) async-start(bf16[16,64,128]{2,1,0:T(8,128)(2,1)} %get-tuple-element.11), calls=%async_computation | async-start | bytes 524288 | tf_op jit(solution)/shard_map/all_to_all | solution.py:261
  28.9 15.9 %collective-permute-start.1 = (bf16[256,1024]{1,0:T(8,128)(2,1)}, bf16[256,1024]{1,0:T(8,128)(2,1)S(1)}, u32[]{:S(2)}, u32[]{:S(2)}) collective-permute-start(bf16[256,1024]{1,0:T(8,128)(2,1)} %get-tuple-element.18), channel_id=1, source_target_pairs={{0,32},{16,48},{32,0},{48,16},{1,33},{17,49},{33,1},{49,17},{2,34}... | collective-permute-start | bytes 1572872 | tf_op jit(solution)/shard_map/ppermute | solution.py:275
  33.3 22.5 %collective-permute-start.2 = (bf16[256,1024]{1,0:T(8,128)(2,1)}, bf16[256,1024]{1,0:T(8,128)(2,1)S(1)}, u32[]{:S(2)}, u32[]{:S(2)}) collective-permute-start(bf16[256,1024]{1,0:T(8,128)(2,1)} %get-tuple-element.19), channel_id=1, source_target_pairs={{0,48},{16,0},{32,16},{48,32},{1,49},{17,1},{33,17},{49,33},{2,50}... | collective-permute-start | bytes 1572872 | tf_op jit(solution)/shard_map/ppermute | solution.py:275
  37.4 0.9 copy-start
  46.8 27.4 %all-to-all-start.1 = ((bf16[8,384,128]{2,1,0:T(8,128)(2,1)}), bf16[8,384,128]{2,1,0:T(8,128)(2,1)S(1)}, u32[]{:S(2)}, u32[]{:S(2)}) async-start(bf16[8,384,128]{2,1,0:T(8,128)(2,1)} %finish.1), calls=%async_computation.1 | async-start | bytes 1572864 | tf_op jit(solution)/shard_map/all_to_all | solution.py:287
  53.7 5.6 %copy-start.4 = (bf16[128,1024]{1,0:T(8,128)(2,1)S(1)}, bf16[128,1024]{1,0:T(8,128)(2,1)}, u32[]{:S(2)}) copy-start(bf16[128,1024]{1,0:T(8,128)(2,1)} %get-tuple-element.23) | copy-start | bytes 786436
  53.7 5.6 %copy-start.5 = (bf16[128,1024]{1,0:T(8,128)(2,1)S(1)}, bf16[128,1024]{1,0:T(8,128)(2,1)}, u32[]{:S(2)}) copy-start(bf16[128,1024]{1,0:T(8,128)(2,1)} %get-tuple-element.25) | copy-start | bytes 786436
  55.9 5.6 %collective-permute-start.3 = (bf16[512,1024]{1,0:T(8,128)(2,1)S(1)}, bf16[512,1024]{1,0:T(8,128)(2,1)S(1)}, u32[]{:S(2)}, u32[]{:S(2)}) collective-permute-start(bf16[512,1024]{1,0:T(8,128)(2,1)S(1)} %pad_maximum_fusion.1), channel_id=1, source_target_pairs={{0,1},{1,0},{2,3},{3,2},{4,5},{5,4},{6,7},{7,6},{8,9},{9,8},{10,11... | collective-permute-start | bytes 3145736 | tf_op jit(solution)/shard_map/ppermute | solution.py:290
  76.2 19.7 %all-to-all-start.2 = ((bf16[8,384,128]{2,1,0:T(8,128)(2,1)}), bf16[8,384,128]{2,1,0:T(8,128)(2,1)S(1)}, u32[]{:S(2)}, u32[]{:S(2)}) async-start(bf16[8,384,128]{2,1,0:T(8,128)(2,1)} %product.1), calls=%async_computation.2 | async-start | bytes 1572864 | tf_op jit(solution)/shard_map/all_to_all | solution.py:300

commit v4 on v2

--- a/solution.py
+++ b/solution.py
@@ -73,14 +73,13 @@
         c.wait()
 
 
-def sort_kernel(shards, rows, fan_x, fan_y, seg_ref, w_ref, *refs):
-    outs, (marks_ref, first_ref, out_sem) = refs[:fan_x], refs[fan_x:]
+def start_cuts(ks, fan_x, fan_y, w_ref, outs, sem):
     feats = w_ref.shape[0]
     width = w_ref.shape[1] // (2 * fan_x * fan_y)
     mine = lax.axis_index("c")
     here = lax.axis_index("x")
     cuts = []
-    for k in reversed(range(fan_x)):
+    for k, out in zip(ks, outs):
         to = lax.rem(here + k, fan_x)
         for y in range(fan_y):
             for other in range(2):
@@ -89,12 +88,23 @@
                 cuts.append(
                     pltpu.make_async_copy(
                         w_ref.at[:, pl.ds(at, width)],
-                        outs[k].at[pl.ds(other * feats, feats), pl.ds(y * width, width)],
-                        out_sem.at[(k * fan_y + y) * 2 + other],
+                        out.at[pl.ds(other * feats, feats), pl.ds(y * width, width)],
+                        sem.at[len(cuts)],
                     )
                 )
     for c in cuts:
         c.start()
+    return cuts
+
+
+def own_kernel(fan_x, fan_y, w_ref, out_ref, sem):
+    for c in start_cuts((0,), fan_x, fan_y, w_ref, (out_ref,), sem):
+        c.wait()
+
+
+def sort_kernel(shards, rows, fan_x, fan_y, seg_ref, w_ref, *refs):
+    outs, (marks_ref, first_ref, out_sem) = refs[: fan_x - 1], refs[fan_x - 1 :]
+    cuts = start_cuts(range(1, fan_x), fan_x, fan_y, w_ref, outs, out_sem)
     for i in range(shards):
         begin = seg_ref[i * rows]
         end = seg_ref[i * rows + rows - 1]
@@ -196,27 +206,30 @@
         c.wait()
 
 
-def product_kernel(fan_x, pay_ref, own_ref, got_ref, out_ref, conv):
-    mine = lax.axis_index("c")
-    here = lax.axis_index("x")
+def product_kernel(fan_x, pay_ref, own_ref, got_ref, keep_ref, give_ref, conv):
     for y in range(pay_ref.shape[0]):
         conv[:, y * LANES : (y + 1) * LANES] = pay_ref[y]
-    for core, w_ref in ((mine, own_ref), (1 - mine, got_ref)):
+    for w_ref, out_ref in ((got_ref, give_ref), (own_ref, keep_ref)):
         for k in range(0, fan_x, 2):
             pair = lax.dot_general(
                 conv[...], w_ref[k * LANES : (k + 2) * LANES, :],
                 (((1,), (1,)), ((), ())), preferred_element_type=F32,
             )
             for n in range(2):
-                to = 2 * lax.rem(here + fan_x - k - n, fan_x) + core
-                out_ref[to] = pair[:, n * LANES : (n + 1) * LANES].astype(BF16)
-
-
-def sum_kernel(parts_ref, out_ref):
-    total = parts_ref[0].astype(F32)
-    for i in range(1, parts_ref.shape[0]):
-        total = total + parts_ref[i].astype(F32)
-    out_ref[...] = total.astype(BF16)
+                part = pair[:, n * LANES : (n + 1) * LANES]
+                out_ref[k + n] = part.astype(out_ref.dtype)
+
+
+def join_kernel(keep_ref, got_ref, *out_refs):
+    for k, out_ref in enumerate(out_refs):
+        out_ref[...] = (keep_ref[k] + got_ref[k].astype(F32)).astype(out_ref.dtype)
+
+
+def sum_kernel(own_ref, *refs):
+    total = own_ref[...]
+    for ref in refs[:-1]:
+        total = total + ref[...].astype(F32)
+    refs[-1][...] = total.astype(BF16)
 
 
 def cost(flops, nbytes):
@@ -254,16 +267,17 @@
         lambda *refs: sort_kernel(shards, rows, fan_x, fan_y, *refs),
         name="sort",
         out_shape=(
-            *(jax.ShapeDtypeStruct((2 * feats, depth), BF16) for _ in range(fan_x)),
+            *(jax.ShapeDtypeStruct((2 * feats, depth), BF16) for _ in range(fan_x - 1)),
             jax.ShapeDtypeStruct((2 * shards, chans), F32),
             jax.ShapeDtypeStruct((SUB, chans), jnp.int32),
         ),
         in_specs=[SM, pl.BlockSpec(memory_space=pltpu.HBM)],
-        out_specs=(VM,) * (fan_x + 2),
-        scratch_shapes=[sem((2 * fan_x * fan_y,))],
+        out_specs=(VM,) * (fan_x + 1),
+        scratch_shapes=[sem((2 * (fan_x - 1) * fan_y,))],
         compiler_params=small,
         cost_estimate=cost(100_000, 4_000_000),
     )(segments, w_in)
+    cuts = [None, *cuts]
     for k in (1, 3, 2):
         cuts[k] = lax.ppermute(cuts[k], "x", [(i, (i + k) % fan_x) for i in range(fan_x)])
     pay = pl.pallas_call(
@@ -278,19 +292,31 @@
         cost_estimate=cost(10_000_000, 1_000_000),
     )(ends_in, marks, residues, decay_rate, base, first)
     pay_in = lax.all_to_all(pay, "y", 0, 0)
+    cuts[0] = pl.pallas_call(
+        lambda *refs: own_kernel(fan_x, fan_y, *refs),
+        name="own",
+        out_shape=jax.ShapeDtypeStruct((2 * feats, depth), BF16),
+        in_specs=[HB], out_specs=VM,
+        scratch_shapes=[sem((2 * fan_y,))],
+        compiler_params=small,
+        cost_estimate=cost(100_000, 1_000_000),
+    )(w_in)
     own = jnp.concatenate([a[:feats] for a in cuts], axis=0)
     give = jnp.concatenate([a[feats:] for a in cuts], axis=0)
     got = lax.ppermute(give, "c", [(0, 1), (1, 0)])
-    split = pl.pallas_call(
+    keep, give = pl.pallas_call(
         lambda *refs: product_kernel(fan_x, *refs),
         name="product",
-        out_shape=jax.ShapeDtypeStruct((2 * fan_x, rows, feats), BF16),
-        in_specs=[VM] * 3, out_specs=VM,
+        out_shape=(
+            jax.ShapeDtypeStruct((fan_x, rows, feats), F32),
+            jax.ShapeDtypeStruct((fan_x, rows, feats), BF16),
+        ),
+        in_specs=[VM] * 3, out_specs=(VM, VM),
         scratch_shapes=[pltpu.VMEM((rows, depth), BF16)],
         compiler_params=small,
         cost_estimate=cost(4 * rows * depth * fan_x * feats, 4_000_000),
     )(pay_in, own, got)
-    split_in = lax.all_to_all(split, ("x", "c"), 0, 0)
+    swapped = lax.ppermute(give, "c", [(0, 1), (1, 0)])
     taps = pl.pallas_call(
         lambda *refs: taps_kernel(rows, *refs),
         name="taps",
@@ -299,14 +325,27 @@
         compiler_params=small,
         cost_estimate=cost(1_000_000, 300_000),
     )(ends_in, marks, decay_rate)
+    parts = pl.pallas_call(
+        join_kernel,
+        name="join",
+        out_shape=tuple(
+            jax.ShapeDtypeStruct((rows, feats), BF16 if k else F32) for k in range(fan_x)
+        ),
+        in_specs=[VM] * 2, out_specs=(VM,) * fan_x,
+        compiler_params=small,
+        cost_estimate=cost(1_000_000, 2_000_000),
+    )(keep, swapped)
+    parts = list(parts)
+    for k in (1, 3, 2):
+        parts[k] = lax.ppermute(parts[k], "x", [(i, (i - k) % fan_x) for i in range(fan_x)])
     d_input = pl.pallas_call(
         sum_kernel,
         name="total",
         out_shape=jax.ShapeDtypeStruct((rows, feats), BF16),
-        in_specs=[VM], out_specs=VM,
+        in_specs=[VM] * fan_x, out_specs=VM,
         compiler_params=small,
         cost_estimate=cost(1_000_000, 900_000),
-    )(split_in)
+    )(*parts)
     return d_input, taps
 
 

time: 104 us -> 102 us (0.981)
  the two profiles are of different devices: /device:TPU:1 before, /device:TPU:64 now
where the time goes in v4:
time: 102 us
  starting transfers between devices  48.8 us (48%)
  waiting for transfers between devices  32 us (31%)
  Pallas kernels  11.5 us (11%)
  local copies, waits for them, and re-layouts  8.36 us (8%)
    all_to_all x1, starting transfers between devices, device(): ends_in = lax.all_to_all(ends, 'z', 0, 0)  18.4 us
    all_to_all x1, waiting for transfers between devices, device(): pay_in = lax.all_to_all(pay, 'y', 0, 0)  15.9 us
    ppermute x3, starting transfers between devices, device(): lax.ppermute(cuts[k], 'x', [(i, (i + k) % fan_x) for i in range(fan_x)])  11.4 us
    ppermute x3, starting transfers between devices, device(): lax.ppermute(parts[k], 'x', [(i, (i - k) % fan_x) for i in range(fan_x)])  8.03 us
    all_to_all x1, starting transfers between devices, device(): pay_in = lax.all_to_all(pay, 'y', 0, 0)  7.11 us
    all_to_all x1, waiting for transfers between devices, device(): ends_in = lax.all_to_all(ends, 'z', 0, 0)  7.09 us
    ppermute x3, waiting for transfers between devices, device(): lax.ppermute(parts[k], 'x', [(i, (i - k) % fan_x) for i in range(fan_x)])  4.75 us
    unnamed x18, local copies, waits for them, and re-layouts  4.74 us
  transfers between devices with their start and end apart: 10, of which 6 were waited for; matrix products, arithmetic and copies ran while one was open for 4% of the time, Pallas kernels for 6%

profile of v4, /device:TPU:64, one launch (start us, length us, event | category | flops | bytes accessed | tf_op | source)
XLA Modules:
  0.0 101.6 jit_solution(11988558412730724976)
XLA Ops:
  0.6 1.6 %copy-done = bf16[128,8192]{1,0:T(8,128)(2,1)S(1)} copy-done((bf16[128,8192]{1,0:T(8,128)(2,1)S(1)}, bf16[128,8192]{1,0:T(8,128)(2,1)}, u32[]{:S(2)}) %copy-start) | copy-done | bytes 2097176
  3.0 3.3 %sort.1 = (bf16[256,1024]{1,0:T(8,128)(2,1)}, bf16[256,1024]{1,0:T(8,128)(2,1)}, bf16[256,1024]{1,0:T(8,128)(2,1)S(1)}, f32[32,128]{1,0:T(8,128)S(1)}, s32[8,128]{1,0:T(8,128)S(1)}) custom-call(s32[6144]{0:T(1024)S(1)} %copy-done.3, bf16[128,8192]{1,0:T(8,128)(2,1)S(1)} %copy-done), custom_call_target="tpu_custom_call" | custom-call | flops 100000 | bytes 4000000 | tf_op jit(solution)/shard_map/sort/pallas_call | solution.py:266
  7.0 3.4 %collective-permute-start = (bf16[256,1024]{1,0:T(8,128)(2,1)}, bf16[256,1024]{1,0:T(8,128)(2,1)}, u32[]{:S(2)}, u32[]{:S(2)}) collective-permute-start(bf16[256,1024]{1,0:T(8,128)(2,1)} %get-tuple-element.19), channel_id=1, source_target_pairs={{0,16},{16,32},{32,48},{48,0},{1,17},{17,33},{33,49},{49,1},{2,18}... | collective-permute-start | bytes 1572872 | tf_op jit(solution)/shard_map/ppermute | solution.py:282
  10.4 4.6 %collective-permute-start.1 = (bf16[256,1024]{1,0:T(8,128)(2,1)}, bf16[256,1024]{1,0:T(8,128)(2,1)}, u32[]{:S(2)}, u32[]{:S(2)}) collective-permute-start(bf16[256,1024]{1,0:T(8,128)(2,1)} %get-tuple-element.20), channel_id=1, source_target_pairs={{0,32},{16,48},{32,0},{48,16},{1,33},{17,49},{33,1},{49,17},{2,34}... | collective-permute-start | bytes 1572872 | tf_op jit(solution)/shard_map/ppermute | solution.py:282
  15.1 4.0 %scan.1 = (bf16[16,48,128]{2,1,0:T(8,128)(2,1)}, f32[384,128]{1,0:T(8,128)}) custom-call(s32[6144]{0:T(1024)} %refs_0_.4, bf16[384,128]{1,0:T(8,128)(2,1)} %refs_1_.2, bf16[384,128]{1,0:T(8,128)(2,1)} %refs_2_.2, f32[16,128]{1,0:T(8,128)} %res_ref.1, f32[16,128]{1,0:T(8,128)} %refs_2_.3), custom_call_target="tpu_custom_call" | custom-call | flops 10000000 | bytes 8000000 | tf_op jit(solution)/shard_map/scan/pallas_call | solution.py:247
  19.1 18.4 %all-to-all-start = ((bf16[16,48,128]{2,1,0:T(8,128)(2,1)}), bf16[16,48,128]{2,1,0:T(8,128)(2,1)S(1)}, u32[]{:S(2)}, u32[]{:S(2)}) async-start(bf16[16,48,128]{2,1,0:T(8,128)(2,1)} %get-tuple-element.15), calls=%async_computation | async-start | bytes 393216 | tf_op jit(solution)/shard_map/all_to_all | solution.py:265
  37.6 3.3 %collective-permute-start.2 = (bf16[256,1024]{1,0:T(8,128)(2,1)}, bf16[256,1024]{1,0:T(8,128)(2,1)S(1)}, u32[]{:S(2)}, u32[]{:S(2)}) collective-permute-start(bf16[256,1024]{1,0:T(8,128)(2,1)} %copy-done.6), channel_id=1, source_target_pairs={{0,48},{16,0},{32,16},{48,32},{1,49},{17,1},{33,17},{49,33},{2,50}... | collective-permute-start | bytes 1572872 | tf_op jit(solution)/shard_map/ppermute | solution.py:282
  40.9 1.6 %copy-done.1 = bf16[128,8192]{1,0:T(8,128)(2,1)S(1)} copy-done((bf16[128,8192]{1,0:T(8,128)(2,1)S(1)}, bf16[128,8192]{1,0:T(8,128)(2,1)}, u32[]{:S(2)}) %copy-start.1) | copy-done | bytes 2097176
  42.9 1.8 %fusion.1 = (bf16[128,1024]{1,0:T(8,128)(2,1)S(1)}, bf16[128,1024]{1,0:T(8,128)(2,1)}) fusion(bf16[256,1024]{1,0:T(8,128)(2,1)} %collective-permute-done), kind=kLoop, calls=%fused_computation.3 | loop fusion | bytes 1048576 | tf_op jit(solution)/shard_map/slice | solution.py:305
  44.7 1.8 %fusion.2 = (bf16[128,1024]{1,0:T(8,128)(2,1)S(1)}, bf16[128,1024]{1,0:T(8,128)(2,1)}) fusion(bf16[256,1024]{1,0:T(8,128)(2,1)} %collective-permute-done.1), kind=kLoop, calls=%fused_computation.4 | loop fusion | bytes 1048576 | tf_op jit(solution)/shard_map/slice | solution.py:305
  46.5 7.1 %all-to-all-done.ends_ref.refs_0_ = bf16[16,48,128]{2,1,0:T(8,128)(2,1)S(1)} async-done(((bf16[16,48,128]{2,1,0:T(8,128)(2,1)}), bf16[16,48,128]{2,1,0:T(8,128)(2,1)S(1)}, u32[]{:S(2)}, u32[]{:S(2)}) %all-to-all-start) | async-done | bytes 196640 | tf_op jit(solution)/shard_map/all_to_all | solution.py:265
  53.6 1.4 %finish.1 = bf16[8,384,128]{2,1,0:T(8,128)(2,1)} custom-call(bf16[16,48,128]{2,1,0:T(8,128)(2,1)S(1)} %all-to-all-done.ends_ref.refs_0_, f32[32,128]{1,0:T(8,128)S(1)} %get-tuple-element.16.marks_ref.refs_1_, f32[16,128]{1,0:T(8,128)S(1)} %copy-done.5, f32[16,128]{1,0:T(8,128)S(1)} %copy-done.4, f32[384,128]{1,0:T(8,128)S(1)} %copy-done.2, ...), custom_call_target="tpu_custom_call" | custom-call | flops 10000000 | bytes 1000000 | tf_op jit(solution)/shard_map/finish/pallas_call | solution.py:283
  55.0 7.1 %all-to-all-start.1 = ((bf16[8,384,128]{2,1,0:T(8,128)(2,1)}), bf16[8,384,128]{2,1,0:T(8,128)(2,1)S(1)}, u32[]{:S(2)}, u32[]{:S(2)}) async-start(bf16[8,384,128]{2,1,0:T(8,128)(2,1)} %finish.1), calls=%async_computation.1 | async-start | bytes 1572864 | tf_op jit(solution)/shard_map/all_to_all | solution.py:294
  62.2 1.9 %collective-permute-start.3 = (bf16[512,1024]{1,0:T(8,128)(2,1)S(1)}, bf16[512,1024]{1,0:T(8,128)(2,1)S(1)}, u32[]{:S(2)}, u32[]{:S(2)}) collective-permute-start(bf16[512,1024]{1,0:T(8,128)(2,1)S(1)} %pad_maximum_fusion.1), channel_id=1, source_target_pairs={{0,1},{1,0},{2,3},{3,2},{4,5},{5,4},{6,7},{7,6},{8,9},{9,8},{10,11... | collective-permute-start | bytes 3145736 | tf_op jit(solution)/shard_map/ppermute | solution.py:306
  64.3 2.5 %collective-permute-done.3.refs_2_ = bf16[512,1024]{1,0:T(8,128)(2,1)S(1)} collective-permute-done((bf16[512,1024]{1,0:T(8,128)(2,1)S(1)}, bf16[512,1024]{1,0:T(8,128)(2,1)S(1)}, u32[]{:S(2)}, u32[]{:S(2)}) %collective-permute-start.3) | collective-permute-done | bytes 1048608 | tf_op jit(solution)/shard_map/ppermute | solution.py:306
  66.8 15.9 %all-to-all-done.1.refs_0_ = bf16[8,384,128]{2,1,0:T(8,128)(2,1)S(1)} async-done(((bf16[8,384,128]{2,1,0:T(8,128)(2,1)}), bf16[8,384,128]{2,1,0:T(8,128)(2,1)S(1)}, u32[]{:S(2)}, u32[]{:S(2)}) %all-to-all-start.1) | async-done | bytes 786464 | tf_op jit(solution)/shard_map/all_to_all | solution.py:294
  82.7 1.0 %product.1 = (f32[4,384,128]{2,1,0:T(8,128)S(1)}, bf16[4,384,128]{2,1,0:T(8,128)(2,1)S(1)}) custom-call(bf16[8,384,128]{2,1,0:T(8,128)(2,1)S(1)} %all-to-all-done.1.refs_0_, bf16[512,1024]{1,0:T(8,128)(2,1)S(1)} %pad_maximum_fusion.refs_1_, bf16[512,1024]{1,0:T(8,128)(2,1)S(1)} %collective-permute-done.3.refs_2_), custom_call_target="tpu_custom_call" | custom-call | flops 805306368 | bytes 4000000 | tf_op jit(solution)/shard_map/product/pallas_call | solution.py:307
  83.8 1.9 %collective-permute-start.4 = (bf16[4,384,128]{2,1,0:T(8,128)(2,1)S(1)}, bf16[4,384,128]{2,1,0:T(8,128)(2,1)S(1)}, u32[]{:S(2)}, u32[]{:S(2)}) collective-permute-start(bf16[4,384,128]{2,1,0:T(8,128)(2,1)S(1)} %get-tuple-element.23), channel_id=1, source_target_pairs={{0,1},{1,0},{2,3},{3,2},{4,5},{5,4},{6,7},{7,6},{8,9},{9,8},{10,11... | collective-permute-start | bytes 1179656 | tf_op jit(solution)/shard_map/ppermute | solution.py:319
  85.7 1.7 %collective-permute-done.4.got_ref = bf16[4,384,128]{2,1,0:T(8,128)(2,1)S(1)} collective-permute-done((bf16[4,384,128]{2,1,0:T(8,128)(2,1)S(1)}, bf16[4,384,128]{2,1,0:T(8,128)(2,1)S(1)}, u32[]{:S(2)}, u32[]{:S(2)}) %collective-permute-start.4) | collective-permute-done | bytes 393248 | tf_op jit(solution)/shard_map/ppermute | solution.py:319
  87.5 3.3 %collective-permute-start.5 = (bf16[384,128]{1,0:T(8,128)(2,1)S(1)}, bf16[384,128]{1,0:T(8,128)(2,1)S(1)}, u32[]{:S(2)}, u32[]{:S(2)}) collective-permute-start(bf16[384,128]{1,0:T(8,128)(2,1)S(1)} %get-tuple-element.25), channel_id=1, source_target_pairs={{0,48},{16,0},{32,16},{48,32},{1,49},{17,1},{33,17},{49,33},{2,50}... | collective-permute-start | bytes 294920 | tf_op jit(solution)/shard_map/ppermute | solution.py:340
  90.8 2.4 %collective-permute-start.6 = (bf16[384,128]{1,0:T(8,128)(2,1)S(1)}, bf16[384,128]{1,0:T(8,128)(2,1)S(1)}, u32[]{:S(2)}, u32[]{:S(2)}) collective-permute-start(bf16[384,128]{1,0:T(8,128)(2,1)S(1)} %get-tuple-element.26), channel_id=1, source_target_pairs={{0,32},{16,48},{32,0},{48,16},{1,33},{17,49},{33,1},{49,17},{2,34}... | collective-permute-start | bytes 294920 | tf_op jit(solution)/shard_map/ppermute | solution.py:340
  93.2 2.3 %collective-permute-start.7 = (bf16[384,128]{1,0:T(8,128)(2,1)S(1)}, bf16[384,128]{1,0:T(8,128)(2,1)S(1)}, u32[]{:S(2)}, u32[]{:S(2)}) collective-permute-start(bf16[384,128]{1,0:T(8,128)(2,1)S(1)} %get-tuple-element.27), channel_id=1, source_target_pairs={{0,16},{16,32},{32,48},{48,0},{1,17},{17,33},{33,49},{49,1},{2,18}... | collective-permute-start | bytes 294920 | tf_op jit(solution)/shard_map/ppermute | solution.py:340
  96.2 2.6 %collective-permute-done.6.refs_1_ = bf16[384,128]{1,0:T(8,128)(2,1)S(1)} collective-permute-done((bf16[384,128]{1,0:T(8,128)(2,1)S(1)}, bf16[384,128]{1,0:T(8,128)(2,1)S(1)}, u32[]{:S(2)}, u32[]{:S(2)}) %collective-permute-start.6) | collective-permute-done | bytes 98336 | tf_op jit(solution)/shard_map/ppermute | solution.py:340
  98.9 2.1 %collective-permute-done.7.refs_2_ = bf16[384,128]{1,0:T(8,128)(2,1)S(1)} collective-permute-done((bf16[384,128]{1,0:T(8,128)(2,1)S(1)}, bf16[384,128]{1,0:T(8,128)(2,1)S(1)}, u32[]{:S(2)}, u32[]{:S(2)}) %collective-permute-start.7) | collective-permute-done | bytes 98336 | tf_op jit(solution)/shard_map/ppermute | solution.py:340
  (28 shorter events, 3.6 us)
Async XLA Ops:
  0.6 1.6 %copy-start = (bf16[128,8192]{1,0:T(8,128)(2,1)S(1)}, bf16[128,8192]{1,0:T(8,128)(2,1)}, u32[]{:S(2)}) copy-start(bf16[128,8192]{1,0:T(8,128)(2,1)} %refs_0_.5) | copy-start | bytes 6291460
  2.2 0.7 copy-start.3
  6.2 0.8 copy-start.6
  7.0 35.9 %collective-permute-start = (bf16[256,1024]{1,0:T(8,128)(2,1)}, bf16[256,1024]{1,0:T(8,128)(2,1)}, u32[]{:S(2)}, u32[]{:S(2)}) collective-permute-start(bf16[256,1024]{1,0:T(8,128)(2,1)} %get-tuple-element.19), channel_id=1, source_target_pairs={{0,16},{16,32},{32,48},{48,0},{1,17},{17,33},{33,49},{49,1},{2,18}... | collective-permute-start | bytes 1572872 | tf_op jit(solution)/shard_map/ppermute | solution.py:282
  10.4 34.3 %collective-permute-start.1 = (bf16[256,1024]{1,0:T(8,128)(2,1)}, bf16[256,1024]{1,0:T(8,128)(2,1)}, u32[]{:S(2)}, u32[]{:S(2)}) collective-permute-start(bf16[256,1024]{1,0:T(8,128)(2,1)} %get-tuple-element.20), channel_id=1, source_target_pairs={{0,32},{16,48},{32,0},{48,16},{1,33},{17,49},{33,1},{49,17},{2,34}... | collective-permute-start | bytes 1572872 | tf_op jit(solution)/shard_map/ppermute | solution.py:282
  19.1 34.5 %all-to-all-start = ((bf16[16,48,128]{2,1,0:T(8,128)(2,1)}), bf16[16,48,128]{2,1,0:T(8,128)(2,1)S(1)}, u32[]{:S(2)}, u32[]{:S(2)}) async-start(bf16[16,48,128]{2,1,0:T(8,128)(2,1)} %get-tuple-element.15), calls=%async_computation | async-start | bytes 393216 | tf_op jit(solution)/shard_map/all_to_all | solution.py:265
  37.6 24.5 %collective-permute-start.2 = (bf16[256,1024]{1,0:T(8,128)(2,1)}, bf16[256,1024]{1,0:T(8,128)(2,1)S(1)}, u32[]{:S(2)}, u32[]{:S(2)}) collective-permute-start(bf16[256,1024]{1,0:T(8,128)(2,1)} %copy-done.6), channel_id=1, source_target_pairs={{0,48},{16,0},{32,16},{48,32},{1,49},{17,1},{33,17},{49,33},{2,50}... | collective-permute-start | bytes 1572872 | tf_op jit(solution)/shard_map/ppermute | solution.py:282
  40.9 1.6 %copy-start.1 = (bf16[128,8192]{1,0:T(8,128)(2,1)S(1)}, bf16[128,8192]{1,0:T(8,128)(2,1)}, u32[]{:S(2)}) copy-start(bf16[128,8192]{1,0:T(8,128)(2,1)} %refs_0_.5) | copy-start | bytes 6291460
  42.9 10.7 %copy-start.2 = (f32[384,128]{1,0:T(8,128)S(1)}, f32[384,128]{1,0:T(8,128)}, u32[]{:S(2)}) copy-start(f32[384,128]{1,0:T(8,128)} %get-tuple-element.17.base_ref) | copy-start | bytes 589828
  42.9 10.7 %copy-start.4 = (f32[16,128]{1,0:T(8,128)S(1)}, f32[16,128]{1,0:T(8,128)}, u32[]{:S(2)}) copy-start(f32[16,128]{1,0:T(8,128)} %refs_2_.3) | copy-start | bytes 24580
  42.9 10.7 %copy-start.5 = (f32[16,128]{1,0:T(8,128)S(1)}, f32[16,128]{1,0:T(8,128)}, u32[]{:S(2)}) copy-start(f32[16,128]{1,0:T(8,128)} %res_ref.1) | copy-start | bytes 24580
  55.0 27.8 %all-to-all-start.1 = ((bf16[8,384,128]{2,1,0:T(8,128)(2,1)}), bf16[8,384,128]{2,1,0:T(8,128)(2,1)S(1)}, u32[]{:S(2)}, u32[]{:S(2)}) async-start(bf16[8,384,128]{2,1,0:T(8,128)(2,1)} %finish.1), calls=%async_computation.1 | async-start | bytes 1572864 | tf_op jit(solution)/shard_map/all_to_all | solution.py:294
  62.1 2.1 %copy-start.7 = (bf16[128,1024]{1,0:T(8,128)(2,1)S(1)}, bf16[128,1024]{1,0:T(8,128)(2,1)}, u32[]{:S(2)}) copy-start(bf16[128,1024]{1,0:T(8,128)(2,1)} %get-tuple-element.31) | copy-start | bytes 786436
  62.1 2.1 %copy-start.8 = (bf16[128,1024]{1,0:T(8,128)(2,1)S(1)}, bf16[128,1024]{1,0:T(8,128)(2,1)}, u32[]{:S(2)}) copy-start(bf16[128,1024]{1,0:T(8,128)(2,1)} %get-tuple-element.33) | copy-start | bytes 786436
  62.2 4.6 %collective-permute-start.3 = (bf16[512,1024]{1,0:T(8,128)(2,1)S(1)}, bf16[512,1024]{1,0:T(8,128)(2,1)S(1)}, u32[]{:S(2)}, u32[]{:S(2)}) collective-permute-start(bf16[512,1024]{1,0:T(8,128)(2,1)S(1)} %pad_maximum_fusion.1), channel_id=1, source_target_pairs={{0,1},{1,0},{2,3},{3,2},{4,5},{5,4},{6,7},{7,6},{8,9},{9,8},{10,11... | collective-permute-start | bytes 3145736 | tf_op jit(solution)/shard_map/ppermute | solution.py:306
  83.8 3.6 %collective-permute-start.4 = (bf16[4,384,128]{2,1,0:T(8,128)(2,1)S(1)}, bf16[4,384,128]{2,1,0:T(8,128)(2,1)S(1)}, u32[]{:S(2)}, u32[]{:S(2)}) collective-permute-start(bf16[4,384,128]{2,1,0:T(8,128)(2,1)S(1)} %get-tuple-element.23), channel_id=1, source_target_pairs={{0,1},{1,0},{2,3},{3,2},{4,5},{5,4},{6,7},{7,6},{8,9},{9,8},{10,11... | collective-permute-start | bytes 1179656 | tf_op jit(solution)/shard_map/ppermute | solution.py:319
  87.5 8.8 %collective-permute-start.5 = (bf16[384,128]{1,0:T(8,128)(2,1)S(1)}, bf16[384,128]{1,0:T(8,128)(2,1)S(1)}, u32[]{:S(2)}, u32[]{:S(2)}) collective-permute-start(bf16[384,128]{1,0:T(8,128)(2,1)S(1)} %get-tuple-element.25), channel_id=1, source_target_pairs={{0,48},{16,0},{32,16},{48,32},{1,49},{17,1},{33,17},{49,33},{2,50}... | collective-permute-start | bytes 294920 | tf_op jit(solution)/shard_map/ppermute | solution.py:340
  90.8 8.0 %collective-permute-start.6 = (bf16[384,128]{1,0:T(8,128)(2,1)S(1)}, bf16[384,128]{1,0:T(8,128)(2,1)S(1)}, u32[]{:S(2)}, u32[]{:S(2)}) collective-permute-start(bf16[384,128]{1,0:T(8,128)(2,1)S(1)} %get-tuple-element.26), channel_id=1, source_target_pairs={{0,32},{16,48},{32,0},{48,16},{1,33},{17,49},{33,1},{49,17},{2,34}... | collective-permute-start | bytes 294920 | tf_op jit(solution)/shard_map/ppermute | solution.py:340
  93.2 7.7 %collective-permute-start.7 = (bf16[384,128]{1,0:T(8,128)(2,1)S(1)}, bf16[384,128]{1,0:T(8,128)(2,1)S(1)}, u32[]{:S(2)}, u32[]{:S(2)}) collective-permute-start(bf16[384,128]{1,0:T(8,128)(2,1)S(1)} %get-tuple-element.27), channel_id=1, source_target_pairs={{0,16},{16,32},{32,48},{48,0},{1,17},{17,33},{33,49},{49,1},{2,18}... | collective-permute-start | bytes 294920 | tf_op jit(solution)/shard_map/ppermute | solution.py:340

commit v5 on v4

--- a/solution.py
+++ b/solution.py
@@ -18,7 +18,7 @@
 
 def scan_kernel(
     shards, seg_ref, g_ref, x_ref, res_ref, rate_ref,
-    ends_ref, base_ref, gf, xf, prod, end_v, end_sem,
+    ends_ref, base_ref, marks_ref, first_ref, gf, xf, prod, end_v, end_sem,
 ):
     rows = g_ref.shape[0]
     base = lax.axis_index("z") * rows
@@ -69,6 +69,26 @@
         return 0
 
     lax.fori_loop(0, rows // 16, fold, 0)
+    for i in range(shards):
+        begin = seg_ref[i * rows]
+        end = seg_ref[i * rows + rows - 1]
+        whole = jnp.where(begin == end, 1.0, 0.0).astype(F32)
+        marks_ref[pl.ds(i, 1), :] = jnp.full((1, LANES), whole, F32)
+        if i + 1 < shards:
+            on = jnp.where(end == seg_ref[(i + 1) * rows], 1.0, 0.0).astype(F32)
+        else:
+            on = jnp.float32(0.0)
+        marks_ref[pl.ds(shards + i, 1), :] = jnp.full((1, LANES), on, F32)
+    last = seg_ref[base + rows - 1]
+
+    def halve(_, span):
+        low, high = span
+        mid = (low + high) // 2
+        inside = seg_ref[base + mid] == last
+        return jnp.where(inside, low, mid + 1), jnp.where(inside, mid, high)
+
+    first, _ = lax.fori_loop(0, rows.bit_length(), halve, (jnp.int32(0), jnp.int32(rows - 1)))
+    first_ref[...] = jnp.full((SUB, LANES), first, jnp.int32)
     for c in ends:
         c.wait()
 
@@ -102,30 +122,8 @@
         c.wait()
 
 
-def sort_kernel(shards, rows, fan_x, fan_y, seg_ref, w_ref, *refs):
-    outs, (marks_ref, first_ref, out_sem) = refs[: fan_x - 1], refs[fan_x - 1 :]
-    cuts = start_cuts(range(1, fan_x), fan_x, fan_y, w_ref, outs, out_sem)
-    for i in range(shards):
-        begin = seg_ref[i * rows]
-        end = seg_ref[i * rows + rows - 1]
-        whole = jnp.where(begin == end, 1.0, 0.0).astype(F32)
-        marks_ref[pl.ds(i, 1), :] = jnp.full((1, LANES), whole, F32)
-        if i + 1 < shards:
-            on = jnp.where(end == seg_ref[(i + 1) * rows], 1.0, 0.0).astype(F32)
-        else:
-            on = jnp.float32(0.0)
-        marks_ref[pl.ds(shards + i, 1), :] = jnp.full((1, LANES), on, F32)
-    start = lax.axis_index("z") * rows
-    last = seg_ref[start + rows - 1]
-
-    def halve(_, span):
-        low, high = span
-        mid = (low + high) // 2
-        inside = seg_ref[start + mid] == last
-        return jnp.where(inside, low, mid + 1), jnp.where(inside, mid, high)
-
-    first, _ = lax.fori_loop(0, rows.bit_length(), halve, (jnp.int32(0), jnp.int32(rows - 1)))
-    first_ref[...] = jnp.full((SUB, LANES), first, jnp.int32)
+def sort_kernel(fan_x, fan_y, w_ref, *refs):
+    cuts = start_cuts(range(1, fan_x), fan_x, fan_y, w_ref, refs[:-1], refs[-1])
     for c in cuts:
         c.wait()
 
@@ -244,15 +242,17 @@
     sem = pltpu.SemaphoreType.DMA
     whole = pltpu.CompilerParams(vmem_limit_bytes=67_000_000)
     small = pltpu.CompilerParams(vmem_limit_bytes=16 * 2**20)
-    ends, base = pl.pallas_call(
+    ends, base, marks, first = pl.pallas_call(
         lambda *refs: scan_kernel(shards, *refs),
         name="scan",
         out_shape=(
             jax.ShapeDtypeStruct((shards, 3 * modes, chans), BF16),
             jax.ShapeDtypeStruct((rows, chans), F32),
+            jax.ShapeDtypeStruct((2 * shards, chans), F32),
+            jax.ShapeDtypeStruct((SUB, chans), jnp.int32),
         ),
         in_specs=[SM, VM, VM, VM, VM],
-        out_specs=(HB, VM),
+        out_specs=(HB, VM, VM, VM),
         scratch_shapes=[
             pltpu.VMEM((rows, chans), F32), pltpu.VMEM((rows, chans), F32),
             pltpu.VMEM((rows * SUB, chans), F32), pltpu.VMEM((3 * modes, chans), BF16),
@@ -263,20 +263,15 @@
     )(segments, out_grad, conv_input, residues, decay_rate)
 
     ends_in = lax.all_to_all(ends, "z", 0, 0)
-    *cuts, marks, first = pl.pallas_call(
-        lambda *refs: sort_kernel(shards, rows, fan_x, fan_y, *refs),
+    cuts = pl.pallas_call(
+        lambda *refs: sort_kernel(fan_x, fan_y, *refs),
         name="sort",
-        out_shape=(
-            *(jax.ShapeDtypeStruct((2 * feats, depth), BF16) for _ in range(fan_x - 1)),
-            jax.ShapeDtypeStruct((2 * shards, chans), F32),
-            jax.ShapeDtypeStruct((SUB, chans), jnp.int32),
-        ),
-        in_specs=[SM, pl.BlockSpec(memory_space=pltpu.HBM)],
-        out_specs=(VM,) * (fan_x + 1),
+        out_shape=tuple(jax.ShapeDtypeStruct((2 * feats, depth), BF16) for _ in range(fan_x - 1)),
+        in_specs=[HB], out_specs=(VM,) * (fan_x - 1),
         scratch_shapes=[sem((2 * (fan_x - 1) * fan_y,))],
         compiler_params=small,
         cost_estimate=cost(100_000, 4_000_000),
-    )(segments, w_in)
+    )(w_in)
     cuts = [None, *cuts]
     for k in (1, 3, 2):
         cuts[k] = lax.ppermute(cuts[k], "x", [(i, (i + k) % fan_x) for i in range(fan_x)])
@@ -336,7 +331,7 @@
         cost_estimate=cost(1_000_000, 2_000_000),
     )(keep, swapped)
     parts = list(parts)
-    for k in (1, 3, 2):
+    for k in (2, 1, 3):
         parts[k] = lax.ppermute(parts[k], "x", [(i, (i - k) % fan_x) for i in range(fan_x)])
     d_input = pl.pallas_call(
         sum_kernel,

time: 102 us -> 100 us (0.980)
  Pallas kernels: 11.5 us -> 10.3 us
    pallas_call x1, Pallas kernels: 3.27 us -> 2.13 us  [device(): pl.pallas_call(lambda *refs: sort_kernel(fan_x, fan_y, *refs), name='sort...]
    unnamed x18 -> x20, local copies, waits for them, and re-layouts: 4.74 us -> 4.03 us
where the time goes in v5:
time: 100 us; the launch traced here: 99.8 us
  starting transfers between devices  48.8 us (49%)
  waiting for transfers between devices  32 us (32%)
  Pallas kernels  10.3 us (10%)
  local copies, waits for them, and re-layouts  7.66 us (8%)
    all_to_all x1, starting transfers between devices, device(): ends_in = lax.all_to_all(ends, 'z', 0, 0)  18.4 us
    all_to_all x1, waiting for transfers between devices, device(): pay_in = lax.all_to_all(pay, 'y', 0, 0)  15.9 us
    ppermute x3, starting transfers between devices, device(): lax.ppermute(cuts[k], 'x', [(i, (i + k) % fan_x) for i in range(fan_x)])  11.4 us
    ppermute x3, starting transfers between devices, device(): lax.ppermute(parts[k], 'x', [(i, (i - k) % fan_x) for i in range(fan_x)])  8.03 us
    all_to_all x1, starting transfers between devices, device(): pay_in = lax.all_to_all(pay, 'y', 0, 0)  7.11 us
    all_to_all x1, waiting for transfers between devices, device(): ends_in = lax.all_to_all(ends, 'z', 0, 0)  7.06 us
    ppermute x3, waiting for transfers between devices, device(): lax.ppermute(parts[k], 'x', [(i, (i - k) % fan_x) for i in range(fan_x)])  4.74 us
    unnamed x20, local copies, waits for them, and re-layouts  4.03 us
  transfers between devices with their start and end apart: 10, of which 6 were waited for; matrix products, arithmetic and copies ran while one was open for 4% of the time, Pallas kernels for 6%

profile of v5, /device:TPU:64, one launch (start us, length us, event | category | flops | bytes accessed | tf_op | source)
XLA Modules:
  0.0 99.8 jit_solution(8576780135876829188)
XLA Ops:
  0.6 1.6 %copy-done = bf16[128,8192]{1,0:T(8,128)(2,1)S(1)} copy-done((bf16[128,8192]{1,0:T(8,128)(2,1)S(1)}, bf16[128,8192]{1,0:T(8,128)(2,1)}, u32[]{:S(2)}) %copy-start) | copy-done | bytes 2097176
  2.2 2.1 %sort.1 = (bf16[256,1024]{1,0:T(8,128)(2,1)}, bf16[256,1024]{1,0:T(8,128)(2,1)}, bf16[256,1024]{1,0:T(8,128)(2,1)S(1)}) custom-call(bf16[128,8192]{1,0:T(8,128)(2,1)S(1)} %copy-done), custom_call_target="tpu_custom_call" | custom-call | flops 100000 | bytes 4000000 | tf_op jit(solution)/shard_map/sort/pallas_call | solution.py:266
  5.2 3.4 %collective-permute-start = (bf16[256,1024]{1,0:T(8,128)(2,1)}, bf16[256,1024]{1,0:T(8,128)(2,1)}, u32[]{:S(2)}, u32[]{:S(2)}) collective-permute-start(bf16[256,1024]{1,0:T(8,128)(2,1)} %get-tuple-element.19), channel_id=1, source_target_pairs={{0,16},{16,32},{32,48},{48,0},{1,17},{17,33},{33,49},{49,1},{2,18}... | collective-permute-start | bytes 1572872 | tf_op jit(solution)/shard_map/ppermute | solution.py:277
  8.6 4.6 %collective-permute-start.1 = (bf16[256,1024]{1,0:T(8,128)(2,1)}, bf16[256,1024]{1,0:T(8,128)(2,1)}, u32[]{:S(2)}, u32[]{:S(2)}) collective-permute-start(bf16[256,1024]{1,0:T(8,128)(2,1)} %get-tuple-element.20), channel_id=1, source_target_pairs={{0,32},{16,48},{32,0},{48,16},{1,33},{17,49},{33,1},{49,17},{2,34}... | collective-permute-start | bytes 1572872 | tf_op jit(solution)/shard_map/ppermute | solution.py:277
  13.2 4.0 %scan.1 = (bf16[16,48,128]{2,1,0:T(8,128)(2,1)}, f32[384,128]{1,0:T(8,128)}, f32[32,128]{1,0:T(8,128)}, s32[8,128]{1,0:T(8,128)}) custom-call(s32[6144]{0:T(1024)} %refs_0_.3, bf16[384,128]{1,0:T(8,128)(2,1)} %refs_1_.1, bf16[384,128]{1,0:T(8,128)(2,1)} %refs_2_.2, f32[16,128]{1,0:T(8,128)} %res_ref.1, f32[16,128]{1,0:T(8,128)} %refs_2_.3), custom_call_target="tpu_custom_call" | custom-call | flops 10000000 | bytes 8000000 | tf_op jit(solution)/shard_map/scan/pallas_call | solution.py:245
  17.3 18.4 %all-to-all-start = ((bf16[16,48,128]{2,1,0:T(8,128)(2,1)}), bf16[16,48,128]{2,1,0:T(8,128)(2,1)S(1)}, u32[]{:S(2)}, u32[]{:S(2)}) async-start(bf16[16,48,128]{2,1,0:T(8,128)(2,1)} %get-tuple-element.15), calls=%async_computation | async-start | bytes 393216 | tf_op jit(solution)/shard_map/all_to_all | solution.py:265
  35.7 3.3 %collective-permute-start.2 = (bf16[256,1024]{1,0:T(8,128)(2,1)}, bf16[256,1024]{1,0:T(8,128)(2,1)S(1)}, u32[]{:S(2)}, u32[]{:S(2)}) collective-permute-start(bf16[256,1024]{1,0:T(8,128)(2,1)} %copy-done.7), channel_id=1, source_target_pairs={{0,48},{16,0},{32,16},{48,32},{1,49},{17,1},{33,17},{49,33},{2,50}... | collective-permute-start | bytes 1572872 | tf_op jit(solution)/shard_map/ppermute | solution.py:277
  39.1 1.6 %copy-done.1 = bf16[128,8192]{1,0:T(8,128)(2,1)S(1)} copy-done((bf16[128,8192]{1,0:T(8,128)(2,1)S(1)}, bf16[128,8192]{1,0:T(8,128)(2,1)}, u32[]{:S(2)}) %copy-start.1) | copy-done | bytes 2097176
  41.1 1.8 %fusion.1 = (bf16[128,1024]{1,0:T(8,128)(2,1)S(1)}, bf16[128,1024]{1,0:T(8,128)(2,1)}) fusion(bf16[256,1024]{1,0:T(8,128)(2,1)} %collective-permute-done), kind=kLoop, calls=%fused_computation.3 | loop fusion | bytes 1048576 | tf_op jit(solution)/shard_map/slice | solution.py:300
  42.9 1.8 %fusion.2 = (bf16[128,1024]{1,0:T(8,128)(2,1)S(1)}, bf16[128,1024]{1,0:T(8,128)(2,1)}) fusion(bf16[256,1024]{1,0:T(8,128)(2,1)} %collective-permute-done.1), kind=kLoop, calls=%fused_computation.4 | loop fusion | bytes 1048576 | tf_op jit(solution)/shard_map/slice | solution.py:300
  44.7 7.1 %all-to-all-done.ends_ref.refs_0_ = bf16[16,48,128]{2,1,0:T(8,128)(2,1)S(1)} async-done(((bf16[16,48,128]{2,1,0:T(8,128)(2,1)}), bf16[16,48,128]{2,1,0:T(8,128)(2,1)S(1)}, u32[]{:S(2)}, u32[]{:S(2)}) %all-to-all-start) | async-done | bytes 196640 | tf_op jit(solution)/shard_map/all_to_all | solution.py:265
  51.8 1.4 %finish.1 = bf16[8,384,128]{2,1,0:T(8,128)(2,1)} custom-call(bf16[16,48,128]{2,1,0:T(8,128)(2,1)S(1)} %all-to-all-done.ends_ref.refs_0_, f32[32,128]{1,0:T(8,128)S(1)} %copy-done.4, f32[16,128]{1,0:T(8,128)S(1)} %copy-done.5, f32[16,128]{1,0:T(8,128)S(1)} %copy-done.3, f32[384,128]{1,0:T(8,128)S(1)} %copy-done.2, s32[8,128]{1,0:T(8,128)S(1)} %copy-done.6), custom_call_target="tpu_custom_call" | custom-call | flops 10000000 | bytes 1000000 | tf_op jit(solution)/shard_map/finish/pallas_call | solution.py:278
  53.1 7.1 %all-to-all-start.1 = ((bf16[8,384,128]{2,1,0:T(8,128)(2,1)}), bf16[8,384,128]{2,1,0:T(8,128)(2,1)S(1)}, u32[]{:S(2)}, u32[]{:S(2)}) async-start(bf16[8,384,128]{2,1,0:T(8,128)(2,1)} %finish.1), calls=%async_computation.1 | async-start | bytes 1572864 | tf_op jit(solution)/shard_map/all_to_all | solution.py:289
  60.4 1.9 %collective-permute-start.3 = (bf16[512,1024]{1,0:T(8,128)(2,1)S(1)}, bf16[512,1024]{1,0:T(8,128)(2,1)S(1)}, u32[]{:S(2)}, u32[]{:S(2)}) collective-permute-start(bf16[512,1024]{1,0:T(8,128)(2,1)S(1)} %pad_maximum_fusion.1), channel_id=1, source_target_pairs={{0,1},{1,0},{2,3},{3,2},{4,5},{5,4},{6,7},{7,6},{8,9},{9,8},{10,11... | collective-permute-start | bytes 3145736 | tf_op jit(solution)/shard_map/ppermute | solution.py:301
  62.4 2.5 %collective-permute-done.3.refs_2_ = bf16[512,1024]{1,0:T(8,128)(2,1)S(1)} collective-permute-done((bf16[512,1024]{1,0:T(8,128)(2,1)S(1)}, bf16[512,1024]{1,0:T(8,128)(2,1)S(1)}, u32[]{:S(2)}, u32[]{:S(2)}) %collective-permute-start.3) | collective-permute-done | bytes 1048608 | tf_op jit(solution)/shard_map/ppermute | solution.py:301
  64.9 15.9 %all-to-all-done.1.refs_0_ = bf16[8,384,128]{2,1,0:T(8,128)(2,1)S(1)} async-done(((bf16[8,384,128]{2,1,0:T(8,128)(2,1)}), bf16[8,384,128]{2,1,0:T(8,128)(2,1)S(1)}, u32[]{:S(2)}, u32[]{:S(2)}) %all-to-all-start.1) | async-done | bytes 786464 | tf_op jit(solution)/shard_map/all_to_all | solution.py:289
  80.9 1.0 %product.1 = (f32[4,384,128]{2,1,0:T(8,128)S(1)}, bf16[4,384,128]{2,1,0:T(8,128)(2,1)S(1)}) custom-call(bf16[8,384,128]{2,1,0:T(8,128)(2,1)S(1)} %all-to-all-done.1.refs_0_, bf16[512,1024]{1,0:T(8,128)(2,1)S(1)} %pad_maximum_fusion.refs_1_, bf16[512,1024]{1,0:T(8,128)(2,1)S(1)} %collective-permute-done.3.refs_2_), custom_call_target="tpu_custom_call" | custom-call | flops 805306368 | bytes 4000000 | tf_op jit(solution)/shard_map/product/pallas_call | solution.py:302
  81.9 1.9 %collective-permute-start.4 = (bf16[4,384,128]{2,1,0:T(8,128)(2,1)S(1)}, bf16[4,384,128]{2,1,0:T(8,128)(2,1)S(1)}, u32[]{:S(2)}, u32[]{:S(2)}) collective-permute-start(bf16[4,384,128]{2,1,0:T(8,128)(2,1)S(1)} %get-tuple-element.23), channel_id=1, source_target_pairs={{0,1},{1,0},{2,3},{3,2},{4,5},{5,4},{6,7},{7,6},{8,9},{9,8},{10,11... | collective-permute-start | bytes 1179656 | tf_op jit(solution)/shard_map/ppermute | solution.py:314
  83.9 1.7 %collective-permute-done.4.got_ref = bf16[4,384,128]{2,1,0:T(8,128)(2,1)S(1)} collective-permute-done((bf16[4,384,128]{2,1,0:T(8,128)(2,1)S(1)}, bf16[4,384,128]{2,1,0:T(8,128)(2,1)S(1)}, u32[]{:S(2)}, u32[]{:S(2)}) %collective-permute-start.4) | collective-permute-done | bytes 393248 | tf_op jit(solution)/shard_map/ppermute | solution.py:314
  85.6 3.3 %collective-permute-start.5 = (bf16[384,128]{1,0:T(8,128)(2,1)S(1)}, bf16[384,128]{1,0:T(8,128)(2,1)S(1)}, u32[]{:S(2)}, u32[]{:S(2)}) collective-permute-start(bf16[384,128]{1,0:T(8,128)(2,1)S(1)} %get-tuple-element.25), channel_id=1, source_target_pairs={{0,48},{16,0},{32,16},{48,32},{1,49},{17,1},{33,17},{49,33},{2,50}... | collective-permute-start | bytes 294920 | tf_op jit(solution)/shard_map/ppermute | solution.py:335
  89.0 2.4 %collective-permute-start.6 = (bf16[384,128]{1,0:T(8,128)(2,1)S(1)}, bf16[384,128]{1,0:T(8,128)(2,1)S(1)}, u32[]{:S(2)}, u32[]{:S(2)}) collective-permute-start(bf16[384,128]{1,0:T(8,128)(2,1)S(1)} %get-tuple-element.26), channel_id=1, source_target_pairs={{0,32},{16,48},{32,0},{48,16},{1,33},{17,49},{33,1},{49,17},{2,34}... | collective-permute-start | bytes 294920 | tf_op jit(solution)/shard_map/ppermute | solution.py:335
  91.4 2.3 %collective-permute-start.7 = (bf16[384,128]{1,0:T(8,128)(2,1)S(1)}, bf16[384,128]{1,0:T(8,128)(2,1)S(1)}, u32[]{:S(2)}, u32[]{:S(2)}) collective-permute-start(bf16[384,128]{1,0:T(8,128)(2,1)S(1)} %get-tuple-element.27), channel_id=1, source_target_pairs={{0,16},{16,32},{32,48},{48,0},{1,17},{17,33},{33,49},{49,1},{2,18}... | collective-permute-start | bytes 294920 | tf_op jit(solution)/shard_map/ppermute | solution.py:335
  94.4 2.6 %collective-permute-done.6.refs_1_ = bf16[384,128]{1,0:T(8,128)(2,1)S(1)} collective-permute-done((bf16[384,128]{1,0:T(8,128)(2,1)S(1)}, bf16[384,128]{1,0:T(8,128)(2,1)S(1)}, u32[]{:S(2)}, u32[]{:S(2)}) %collective-permute-start.6) | collective-permute-done | bytes 98336 | tf_op jit(solution)/shard_map/ppermute | solution.py:335
  97.0 2.1 %collective-permute-done.7.refs_2_ = bf16[384,128]{1,0:T(8,128)(2,1)S(1)} collective-permute-done((bf16[384,128]{1,0:T(8,128)(2,1)S(1)}, bf16[384,128]{1,0:T(8,128)(2,1)S(1)}, u32[]{:S(2)}, u32[]{:S(2)}) %collective-permute-start.7) | collective-permute-done | bytes 98336 | tf_op jit(solution)/shard_map/ppermute | solution.py:335
  (30 shorter events, 2.9 us)
Async XLA Ops:
  0.6 1.6 %copy-start = (bf16[128,8192]{1,0:T(8,128)(2,1)S(1)}, bf16[128,8192]{1,0:T(8,128)(2,1)}, u32[]{:S(2)}) copy-start(bf16[128,8192]{1,0:T(8,128)(2,1)} %refs_0_.5) | copy-start | bytes 6291460
  4.4 0.8 copy-start.7
  5.2 35.9 %collective-permute-start = (bf16[256,1024]{1,0:T(8,128)(2,1)}, bf16[256,1024]{1,0:T(8,128)(2,1)}, u32[]{:S(2)}, u32[]{:S(2)}) collective-permute-start(bf16[256,1024]{1,0:T(8,128)(2,1)} %get-tuple-element.19), channel_id=1, source_target_pairs={{0,16},{16,32},{32,48},{48,0},{1,17},{17,33},{33,49},{49,1},{2,18}... | collective-permute-start | bytes 1572872 | tf_op jit(solution)/shard_map/ppermute | solution.py:277
  8.6 34.3 %collective-permute-start.1 = (bf16[256,1024]{1,0:T(8,128)(2,1)}, bf16[256,1024]{1,0:T(8,128)(2,1)}, u32[]{:S(2)}, u32[]{:S(2)}) collective-permute-start(bf16[256,1024]{1,0:T(8,128)(2,1)} %get-tuple-element.20), channel_id=1, source_target_pairs={{0,32},{16,48},{32,0},{48,16},{1,33},{17,49},{33,1},{49,17},{2,34}... | collective-permute-start | bytes 1572872 | tf_op jit(solution)/shard_map/ppermute | solution.py:277
  17.3 34.5 %all-to-all-start = ((bf16[16,48,128]{2,1,0:T(8,128)(2,1)}), bf16[16,48,128]{2,1,0:T(8,128)(2,1)S(1)}, u32[]{:S(2)}, u32[]{:S(2)}) async-start(bf16[16,48,128]{2,1,0:T(8,128)(2,1)} %get-tuple-element.15), calls=%async_computation | async-start | bytes 393216 | tf_op jit(solution)/shard_map/all_to_all | solution.py:265
  35.7 24.5 %collective-permute-start.2 = (bf16[256,1024]{1,0:T(8,128)(2,1)}, bf16[256,1024]{1,0:T(8,128)(2,1)S(1)}, u32[]{:S(2)}, u32[]{:S(2)}) collective-permute-start(bf16[256,1024]{1,0:T(8,128)(2,1)} %copy-done.7), channel_id=1, source_target_pairs={{0,48},{16,0},{32,16},{48,32},{1,49},{17,1},{33,17},{49,33},{2,50}... | collective-permute-start | bytes 1572872 | tf_op jit(solution)/shard_map/ppermute | solution.py:277
  39.1 1.6 %copy-start.1 = (bf16[128,8192]{1,0:T(8,128)(2,1)S(1)}, bf16[128,8192]{1,0:T(8,128)(2,1)}, u32[]{:S(2)}) copy-start(bf16[128,8192]{1,0:T(8,128)(2,1)} %refs_0_.5) | copy-start | bytes 6291460
  41.0 10.7 %copy-start.2 = (f32[384,128]{1,0:T(8,128)S(1)}, f32[384,128]{1,0:T(8,128)}, u32[]{:S(2)}) copy-start(f32[384,128]{1,0:T(8,128)} %get-tuple-element.17.base_ref) | copy-start | bytes 589828
  41.0 10.7 %copy-start.3 = (f32[16,128]{1,0:T(8,128)S(1)}, f32[16,128]{1,0:T(8,128)}, u32[]{:S(2)}) copy-start(f32[16,128]{1,0:T(8,128)} %refs_2_.3) | copy-start | bytes 24580
  41.0 10.7 %copy-start.4 = (f32[32,128]{1,0:T(8,128)S(1)}, f32[32,128]{1,0:T(8,128)}, u32[]{:S(2)}) copy-start(f32[32,128]{1,0:T(8,128)} %get-tuple-element.16.marks_ref.refs_1_) | copy-start | bytes 49156
  41.0 10.7 %copy-start.5 = (f32[16,128]{1,0:T(8,128)S(1)}, f32[16,128]{1,0:T(8,128)}, u32[]{:S(2)}) copy-start(f32[16,128]{1,0:T(8,128)} %res_ref.1) | copy-start | bytes 24580
  41.0 10.7 %copy-start.6 = (s32[8,128]{1,0:T(8,128)S(1)}, s32[8,128]{1,0:T(8,128)}, u32[]{:S(2)}) copy-start(s32[8,128]{1,0:T(8,128)} %get-tuple-element.18.first_ref) | copy-start | bytes 12292
  53.1 27.8 %all-to-all-start.1 = ((bf16[8,384,128]{2,1,0:T(8,128)(2,1)}), bf16[8,384,128]{2,1,0:T(8,128)(2,1)S(1)}, u32[]{:S(2)}, u32[]{:S(2)}) async-start(bf16[8,384,128]{2,1,0:T(8,128)(2,1)} %finish.1), calls=%async_computation.1 | async-start | bytes 1572864 | tf_op jit(solution)/shard_map/all_to_all | solution.py:289
  60.2 2.1 %copy-start.8 = (bf16[128,1024]{1,0:T(8,128)(2,1)S(1)}, bf16[128,1024]{1,0:T(8,128)(2,1)}, u32[]{:S(2)}) copy-start(bf16[128,1024]{1,0:T(8,128)(2,1)} %get-tuple-element.31) | copy-start | bytes 786436
  60.2 2.1 %copy-start.9 = (bf16[128,1024]{1,0:T(8,128)(2,1)S(1)}, bf16[128,1024]{1,0:T(8,128)(2,1)}, u32[]{:S(2)}) copy-start(bf16[128,1024]{1,0:T(8,128)(2,1)} %get-tuple-element.33) | copy-start | bytes 786436
  60.4 4.6 %collective-permute-start.3 = (bf16[512,1024]{1,0:T(8,128)(2,1)S(1)}, bf16[512,1024]{1,0:T(8,128)(2,1)S(1)}, u32[]{:S(2)}, u32[]{:S(2)}) collective-permute-start(bf16[512,1024]{1,0:T(8,128)(2,1)S(1)} %pad_maximum_fusion.1), channel_id=1, source_target_pairs={{0,1},{1,0},{2,3},{3,2},{4,5},{5,4},{6,7},{7,6},{8,9},{9,8},{10,11... | collective-permute-start | bytes 3145736 | tf_op jit(solution)/shard_map/ppermute | solution.py:301
  81.9 3.6 %collective-permute-start.4 = (bf16[4,384,128]{2,1,0:T(8,128)(2,1)S(1)}, bf16[4,384,128]{2,1,0:T(8,128)(2,1)S(1)}, u32[]{:S(2)}, u32[]{:S(2)}) collective-permute-start(bf16[4,384,128]{2,1,0:T(8,128)(2,1)S(1)} %get-tuple-element.23), channel_id=1, source_target_pairs={{0,1},{1,0},{2,3},{3,2},{4,5},{5,4},{6,7},{7,6},{8,9},{9,8},{10,11... | collective-permute-start | bytes 1179656 | tf_op jit(solution)/shard_map/ppermute | solution.py:314
  85.6 8.8 %collective-permute-start.5 = (bf16[384,128]{1,0:T(8,128)(2,1)S(1)}, bf16[384,128]{1,0:T(8,128)(2,1)S(1)}, u32[]{:S(2)}, u32[]{:S(2)}) collective-permute-start(bf16[384,128]{1,0:T(8,128)(2,1)S(1)} %get-tuple-element.25), channel_id=1, source_target_pairs={{0,48},{16,0},{32,16},{48,32},{1,49},{17,1},{33,17},{49,33},{2,50}... | collective-permute-start | bytes 294920 | tf_op jit(solution)/shard_map/ppermute | solution.py:335
  89.0 8.0 %collective-permute-start.6 = (bf16[384,128]{1,0:T(8,128)(2,1)S(1)}, bf16[384,128]{1,0:T(8,128)(2,1)S(1)}, u32[]{:S(2)}, u32[]{:S(2)}) collective-permute-start(bf16[384,128]{1,0:T(8,128)(2,1)S(1)} %get-tuple-element.26), channel_id=1, source_target_pairs={{0,32},{16,48},{32,0},{48,16},{1,33},{17,49},{33,1},{49,17},{2,34}... | collective-permute-start | bytes 294920 | tf_op jit(solution)/shard_map/ppermute | solution.py:335
  91.4 7.7 %collective-permute-start.7 = (bf16[384,128]{1,0:T(8,128)(2,1)S(1)}, bf16[384,128]{1,0:T(8,128)(2,1)S(1)}, u32[]{:S(2)}, u32[]{:S(2)}) collective-permute-start(bf16[384,128]{1,0:T(8,128)(2,1)S(1)} %get-tuple-element.27), channel_id=1, source_target_pairs={{0,16},{16,32},{32,48},{48,0},{1,17},{17,33},{33,49},{49,1},{2,18}... | collective-permute-start | bytes 294920 | tf_op jit(solution)/shard_map/ppermute | solution.py:335
